TPU v7x, 32 devices: a whole 2x2x4 slice. The times are simulated.
32 devices in a mesh: gx: 8 (over z, x), gy: 4 (over y, core).
Axes of the slice: x: 2, y: 2, z: 4, core: 2. Of those that a mesh axis runs over, the one named last changes fastest.
Arguments:
- e_start: float32 [3, 64, 256, 128], P(None, 'gx', 'gy'), may hold values from -6 to 6
- h_start: float32 [3, 64, 256, 128], P(None, 'gx', 'gy'), may hold values from -6 to 6
- adj_e_start: float32 [3, 64, 256, 128], P(None, 'gx', 'gy'), may hold values from -6 to 6
- adj_h_start: float32 [3, 64, 256, 128], P(None, 'gx', 'gy'), may hold values from -6 to 6
- eps_background: float32 [64, 256, 128], P('gx', 'gy'), may hold values from 1 to 4
- design: float32 [64, 256], P('gx', 'gy'), may hold values from 0 to 1
- design_tiles: int32 [8, 32], P('gx', 'gy'), may hold values from 0 to 1
- design_floor: int32 [1], replicated, may hold values from 8 to 104
- freq_index: int32 [8], replicated, may hold values from 0 to 31, as said below
- target: float32 [2, 8, 3, 64, 256], P(None, None, None, 'gx', 'gy'), may hold values from -6 to 6
Outputs:
- grad_design: float32 [64, 256], P('gx', 'gy')
- loss_weights: float32 [8], replicated
- e_final: float32 [3, 64, 256, 128], P(None, 'gx', 'gy')
- adj_e_final: float32 [3, 64, 256, 128], P(None, 'gx', 'gy')
Inputs may be any that keep to these rules, and one draw needn't show every extreme that they name: `freq_index`: 8 distinct entries; the first and the last entry of the table are always among them.
All inputs are finite; a program needn't handle non-finite values.
Results may differ from a plain program's by a relative error of at most 0.00018.
Values sent between devices are 32-bit elements; how exact they have to be, the bound alone decides.
A program may use at most 64 MiB of HBM per device.

v0:
```python
import jax
import jax.numpy as jnp
from jax import lax
from jax.sharding import PartitionSpec as P

STEPS = 4
DZ = 16
TILE = 8


courant = 0.5
sharpness = 4.0
contrast = 10.0
threshold = 0.5


def with_halo(block, sides, width):
    for axis, dim in sides:
        count = lax.axis_size(axis)
        forward = [(i, i + 1) for i in range(count - 1)]
        backward = [(target, source) for source, target in forward]
        low = lax.ppermute(
            lax.slice_in_dim(block, block.shape[dim] - width, None, axis=dim), axis, forward
        )
        high = lax.ppermute(lax.slice_in_dim(block, 0, width, axis=dim), axis, backward)
        block = jnp.concatenate([low, block, high], axis=dim)
    return block


def step_ahead(values, face_cells, along_axis):
    shifted = lax.slice_in_dim(values, 1, values.shape[along_axis], axis=along_axis)
    return jnp.concatenate([shifted, face_cells], along_axis) - values


def behind(values, face_cells, along_axis):
    shifted = lax.slice_in_dim(values, 0, values.shape[along_axis] - 1, axis=along_axis)
    return values - jnp.concatenate([face_cells, shifted], along_axis)


def zero_face(values, along_axis):
    return jnp.zeros_like(lax.slice_in_dim(values, 0, 1, axis=along_axis))


def curl_ahead(e_field, ey_face_x, ez_face_x, ex_face_y, ez_face_y):
    e_x, e_y, e_z = (e_field[0], e_field[1], e_field[2])
    curl_x = step_ahead(e_z, ez_face_y, 1) - step_ahead(e_y, zero_face(e_y, 2), 2)
    curl_y = step_ahead(e_x, zero_face(e_x, 2), 2) - step_ahead(e_z, ez_face_x, 0)
    curl_z = step_ahead(e_y, ey_face_x, 0) - step_ahead(e_x, ex_face_y, 1)
    return jnp.stack([curl_x, curl_y, curl_z])


def curl_behind(h_field, hy_face_x, hz_face_x, hx_face_y, hz_face_y):
    h_x, h_y, h_z = (h_field[0], h_field[1], h_field[2])
    curl_x = behind(h_z, hz_face_y, 1) - behind(h_y, zero_face(h_y, 2), 2)
    curl_y = behind(h_x, zero_face(h_x, 2), 2) - behind(h_z, hz_face_x, 0)
    curl_z = behind(h_y, hy_face_x, 0) - behind(h_x, hx_face_y, 1)
    return jnp.stack([curl_x, curl_y, curl_z])


def smooth_padded(extended):
    row_count = extended.shape[0] - 4
    first_pass = (
        extended[0:row_count]
        + 2.0 * extended[1 : row_count + 1]
        + 3.0 * extended[2 : row_count + 2]
        + 2.0 * extended[3 : row_count + 3]
        + extended[4 : row_count + 4]
    ) / 9.0
    col_count = first_pass.shape[1] - 4
    return (
        first_pass[:, 0:col_count]
        + 2.0 * first_pass[:, 1 : col_count + 1]
        + 3.0 * first_pass[:, 2 : col_count + 2]
        + 2.0 * first_pass[:, 3 : col_count + 3]
        + first_pass[:, 4 : col_count + 4]
    ) / 9.0


def cell_mask(tile_flags):
    spread = tile_flags.astype(jnp.float32)[:, None, :, None] * jnp.ones(
        (1, TILE, 1, TILE), jnp.float32
    )
    return spread.reshape(tile_flags.shape[0] * TILE, tile_flags.shape[1] * TILE)


def open_faces(field):
    return (
        zero_face(field[1], 0),
        zero_face(field[2], 0),
        zero_face(field[0], 1),
        zero_face(field[2], 1),
    )


def extend_fields(both_fields):
    return with_halo(both_fields, (("gx", 1), ("gy", 2)), STEPS)


def start_sums(freq_count, rows_x, rows_y):
    slab_re = jnp.zeros((freq_count, 3, rows_x, rows_y * DZ), jnp.float32)
    slab_im = jnp.zeros((freq_count, 3, rows_x, rows_y * DZ), jnp.float32)
    watch_re = jnp.zeros((freq_count, 3, rows_x, rows_y), jnp.float32)
    watch_im = jnp.zeros((freq_count, 3, rows_x, rows_y), jnp.float32)
    return (slab_re, slab_im, watch_re, watch_im)


def add_transforms(sums, e_own, cosines, sines, z_floor):
    slab_re, slab_im, watch_re, watch_im = sums
    rows_x, rows_y = (e_own.shape[1], e_own.shape[2])
    slab_cells = lax.dynamic_slice_in_dim(e_own, z_floor, DZ, 3).reshape(3, rows_x, rows_y * DZ)
    monitor_cells = lax.dynamic_index_in_dim(e_own, z_floor + DZ, 3, keepdims=False)
    slab_re = slab_re + cosines[:, None, None, None] * slab_cells[None]
    slab_im = slab_im - sines[:, None, None, None] * slab_cells[None]
    watch_re = watch_re + cosines[:, None, None, None] * monitor_cells[None]
    watch_im = watch_im - sines[:, None, None, None] * monitor_cells[None]
    return (slab_re, slab_im, watch_re, watch_im)


def window(
    e_field, h_field, scale_wide, inside_wide, angular, z_floor, source_layer, adjoint_source
):
    rows_x, rows_y = (e_field.shape[1], e_field.shape[2])
    sums = start_sums(angular.shape[0], rows_x, rows_y)
    wide = extend_fields(jnp.concatenate([e_field, h_field], 0))
    e_wide = wide[:3]
    h_wide = wide[3:]
    source_wide = None
    if adjoint_source is not None:
        planes = []
        for step_index in range(STEPS):
            time_value = jnp.float32(step_index + 1)
            planes.append(
                adjoint_source(jnp.cos(angular * time_value), jnp.sin(angular * time_value))
            )
        source_wide = with_halo(jnp.stack(planes), (("gx", 2), ("gy", 3)), STEPS)
    e_own = e_field
    for step_index in range(STEPS):
        h_wide = (h_wide - courant * curl_ahead(e_wide, *open_faces(e_wide))) * inside_wide
        e_wide = e_wide + scale_wide[None] * curl_behind(h_wide, *open_faces(h_wide))
        time_value = jnp.float32(step_index + 1)
        cosines = jnp.cos(angular * time_value)
        sines = jnp.sin(angular * time_value)
        if source_wide is not None:
            e_wide = e_wide + source_wide[step_index][..., None] * source_layer
        e_own = e_wide[:, STEPS : STEPS + rows_x, STEPS : STEPS + rows_y]
        sums = add_transforms(sums, e_own, cosines, sines, z_floor)
    return (sums[0], sums[1], sums[2], sums[3], e_own)


def body(
    e_start,
    h_start,
    adj_e_start,
    adj_h_start,
    eps_background,
    design,
    design_tiles,
    design_floor,
    freq_index,
    target,
):
    z_floor = design_floor[0]
    rows_x, rows_y = (e_start.shape[1], e_start.shape[2])
    layers = lax.iota(jnp.int32, e_start.shape[3])
    source_layer = (layers == z_floor + DZ).astype(jnp.float32)
    design_layers = ((layers >= z_floor) & (layers < z_floor + DZ)).astype(jnp.float32)
    tile_cells = cell_mask(design_tiles)
    extended = with_halo(design, (("gx", 0), ("gy", 1)), 2)
    filtered = smooth_padded(extended)
    tilted = jnp.tanh(sharpness * (filtered - threshold))
    offset_tanh = jnp.tanh(sharpness * threshold)
    projected = (offset_tanh + tilted) / (2.0 * offset_tanh)
    gradient_slope = sharpness * (1.0 - tilted * tilted) / (2.0 * offset_tanh)
    inside = tile_cells[:, :, None] * design_layers
    permittivity = jnp.where(inside > 0.5, 1.0 + contrast * projected[:, :, None], eps_background)
    update_scale = courant / permittivity
    scale_wide = None
    inside_wide = None
    scale_wide = with_halo(update_scale, (("gx", 0), ("gy", 1)), STEPS)
    global_x = lax.axis_index("gx") * rows_x + lax.iota(jnp.int32, rows_x + 2 * STEPS) - STEPS
    global_y = lax.axis_index("gy") * rows_y + lax.iota(jnp.int32, rows_y + 2 * STEPS) - STEPS
    within_x = (global_x >= 0) & (global_x < rows_x * lax.axis_size("gx"))
    within_y = (global_y >= 0) & (global_y < rows_y * lax.axis_size("gy"))
    inside_wide = (within_x[:, None] & within_y[None, :]).astype(jnp.float32)[:, :, None]
    angular = 0.3 + 0.04 * freq_index.astype(jnp.float32)
    fwd_re, fwd_im, watch_re, watch_im, e_final = window(
        e_start, h_start, scale_wide, inside_wide, angular, z_floor, source_layer, None
    )
    misfit_re = watch_re - target[0]
    misfit_im = watch_im - target[1]
    local_sums = jnp.sum(misfit_re * misfit_re + misfit_im * misfit_im, axis=(1, 2, 3))
    loss_sums = lax.psum(local_sums, ("gx", "gy"))
    cell_count = 3 * rows_x * lax.axis_size("gx") * rows_y * lax.axis_size("gy")
    losses = loss_sums / float(cell_count) + 1e-06
    squared = losses * losses
    weights = squared / jnp.sum(squared)

    def adjoint_source(cosines, sines):
        first = jnp.einsum(
            "k,kcxy->cxy", weights * cosines, misfit_re, precision=lax.Precision.HIGHEST
        )
        second = jnp.einsum(
            "k,kcxy->cxy", weights * sines, misfit_im, precision=lax.Precision.HIGHEST
        )
        return first - second

    adj_re, adj_im, unused_re, unused_im, adj_e_final = window(
        adj_e_start,
        adj_h_start,
        scale_wide,
        inside_wide,
        angular,
        z_floor,
        source_layer,
        adjoint_source,
    )
    product = fwd_re * adj_re - fwd_im * adj_im
    density = jnp.einsum("k,kcxw->xw", weights, product, precision=lax.Precision.HIGHEST)
    sensitivity = jnp.sum(density.reshape(rows_x, rows_y, DZ), axis=2) / float(3 * DZ)
    grad_extended = with_halo(tile_cells * gradient_slope * sensitivity, (("gx", 0), ("gy", 1)), 2)
    return (smooth_padded(grad_extended), weights, e_final, adj_e_final)


def solution(mesh):
    placed = (
        P(None, "gx", "gy", None),
        P(None, "gx", "gy", None),
        P(None, "gx", "gy", None),
        P(None, "gx", "gy", None),
        P("gx", "gy", None),
        P("gx", "gy"),
        P("gx", "gy"),
        P(),
        P(),
        P(None, None, None, "gx", "gy"),
    )
    return jax.shard_map(
        body,
        mesh=mesh,
        in_specs=placed,
        out_specs=(P("gx", "gy"), P(), P(None, "gx", "gy", None), P(None, "gx", "gy", None)),
        check_vma=False,
    )
```

profile of v0, /device:TPU:1, one launch (start us, length us, event | category | flops | bytes accessed | tf_op | source)
XLA Modules:
  0.0 258.9 jit_solution(13673220521744659239)
XLA Ops:
  1.4 3.9 %collective-permute-start = (f32[2,64]{1,0:T(2,128)S(1)}, f32[2,64]{1,0:T(2,128)S(1)}, u32[]{:S(2)}, u32[]{:S(2)}) collective-permute-start(f32[2,64]{1,0:T(2,128)S(1)} %get-tuple-element.181), channel_id=1, source_target_pairs={{0,4},{4,8},{8,12},{12,16},{16,20},{20,24},{24,28},{1,5},{5,9},{9,... | collective-permute-start | bytes 1544 | tf_op jit(solution)/shard_map/ppermute | solution.py:22
  5.4 1.3 collective-permute-start.1
  6.7 1.2 constant_dynamic-update-slice_fusion.3
  8.0 1.3 fusion.76
  9.3 4.9 %collective-permute-start.12 = (f32[6,4,64,128]{3,2,1,0:T(8,128)}, f32[6,4,64,128]{3,2,1,0:T(8,128)}, u32[]{:S(2)}, u32[]{:S(2)}) collective-permute-start(f32[6,4,64,128]{3,2,1,0:T(8,128)} %get-tuple-element.159), channel_id=1, source_target_pairs={{0,4},{4,8},{8,12},{12,16},{16,20},{20,24},{24,28},{1,5},{5,9},{9,... | collective-permute-start | bytes 2359304 | tf_op jit(solution)/shard_map/ppermute | solution.py:22
  14.1 1.3 collective-permute-start.13
  15.6 1.2 fusion.75
  16.9 4.9 %collective-permute-start.4 = (f32[6,4,64,128]{3,2,1,0:T(8,128)}, f32[6,4,64,128]{3,2,1,0:T(8,128)}, u32[]{:S(2)}, u32[]{:S(2)}) collective-permute-start(f32[6,4,64,128]{3,2,1,0:T(8,128)} %get-tuple-element.157), channel_id=1, source_target_pairs={{0,4},{4,8},{8,12},{12,16},{16,20},{20,24},{24,28},{1,5},{5,9},{9,... | collective-permute-start | bytes 2359304 | tf_op jit(solution)/shard_map/ppermute | solution.py:22
  22.8 5.1 %collective-permute-start.2 = (f32[12,2]{1,0:T(8,128)S(1)}, f32[12,2]{1,0:T(8,128)S(1)}, u32[]{:S(2)}, u32[]{:S(2)}) collective-permute-start(f32[12,2]{1,0:T(8,128)S(1)} %get-tuple-element.177), channel_id=1, source_target_pairs={{0,1},{1,2},{2,3},{4,5},{5,6},{6,7},{8,9},{9,10},{10,11},{12,13},{... | collective-permute-start | bytes 296 | tf_op jit(solution)/shard_map/ppermute | solution.py:22
  27.9 1.9 collective-permute-start.3
  29.9 1.3 collective-permute-start.5
  31.2 2.1 collective-permute-done.3
  34.1 1.1 select_divide_fusion
  35.9 3.2 %collective-permute-start.8 = (f32[4,64,128]{2,1,0:T(8,128)S(1)}, f32[4,64,128]{2,1,0:T(8,128)S(1)}, u32[]{:S(2)}, u32[]{:S(2)}) collective-permute-start(f32[4,64,128]{2,1,0:T(8,128)S(1)} %get-tuple-element.163), channel_id=1, source_target_pairs={{0,4},{4,8},{8,12},{12,16},{16,20},{20,24},{24,28},{1,5},{5,9},{9,... | collective-permute-start | bytes 393224 | tf_op jit(solution)/shard_map/ppermute | solution.py:22
  39.7 42.7 %collective-permute-done.8 = f32[4,64,128]{2,1,0:T(8,128)S(1)} collective-permute-done((f32[4,64,128]{2,1,0:T(8,128)S(1)}, f32[4,64,128]{2,1,0:T(8,128)S(1)}, u32[]{:S(2)}, u32[]{:S(2)}) %collective-permute-start.8) | collective-permute-done | bytes 131104 | tf_op jit(solution)/shard_map/ppermute | solution.py:22
  82.4 1.3 collective-permute-start.9
  83.7 1.2 broadcast_multiply_fusion
  85.5 3.8 %collective-permute-done.9 = f32[4,64,128]{2,1,0:T(8,128)} collective-permute-done((f32[4,64,128]{2,1,0:T(8,128)}, f32[4,64,128]{2,1,0:T(8,128)}, u32[]{:S(2)}, u32[]{:S(2)}) %collective-permute-start.9) | collective-permute-done | bytes 131104 | tf_op jit(solution)/shard_map/ppermute | solution.py:25
  90.0 6.0 %collective-permute-start.10 = (f32[16,4,128]{2,1,0:T(4,128)S(1)}, f32[16,4,128]{2,1,0:T(4,128)S(1)}, u32[]{:S(2)}, u32[]{:S(2)}) collective-permute-start(f32[16,4,128]{2,1,0:T(4,128)S(1)} %get-tuple-element.161), channel_id=1, source_target_pairs={{0,1},{1,2},{2,3},{4,5},{5,6},{6,7},{8,9},{9,10},{10,11},{12,13},{... | collective-permute-start | bytes 98312 | tf_op jit(solution)/shard_map/ppermute | solution.py:22
  96.0 1.9 collective-permute-start.11
  98.0 1.1 pad_maximum_fusion.12
  99.1 1.9 collective-permute-start.7
  101.1 3.6 %collective-permute-start.6 = (f32[6,16,4,128]{3,1,2,0:T(8,128)S(1)}, f32[6,16,4,128]{3,1,2,0:T(8,128)S(1)}, u32[]{:S(2)}, u32[]{:S(2)}) collective-permute-start(f32[6,16,4,128]{3,1,2,0:T(8,128)S(1)} %copy.158), channel_id=1, source_target_pairs={{0,1},{1,2},{2,3},{4,5},{5,6},{6,7},{8,9},{9,10},{10,11},{12,13},{... | collective-permute-start | bytes 589832 | tf_op jit(solution)/shard_map/ppermute | solution.py:22
  105.8 1.2 pad_maximum_fusion.9
  107.1 1.9 collective-permute-start.15
  109.0 3.6 %collective-permute-start.14 = (f32[6,16,4,128]{3,1,2,0:T(8,128)S(1)}, f32[6,16,4,128]{3,1,2,0:T(8,128)S(1)}, u32[]{:S(2)}, u32[]{:S(2)}) collective-permute-start(f32[6,16,4,128]{3,1,2,0:T(8,128)S(1)} %copy.162), channel_id=1, source_target_pairs={{0,1},{1,2},{2,3},{4,5},{5,6},{6,7},{8,9},{9,10},{10,11},{12,13},{... | collective-permute-start | bytes 589832 | tf_op jit(solution)/shard_map/ppermute | solution.py:22
  112.8 1.9 pad_maximum_fusion
  124.0 1.9 pad_maximum_fusion.1
  127.7 1.2 fusion.10
  128.8 1.1 slice_bitcast_fusion.61
  130.0 1.3 slice_bitcast_fusion.20
  135.2 39.6 %psum.7 = f32[8]{0:T(128)S(1)} all-reduce(f32[8]{0:T(128)} %get-tuple-element.16), channel_id=1, replica_groups=mesh['gx'=8,'gy'=4] {'gx','gy'}, use_global_device_ids=true, to_apply=%region_1.2 | all-reduce | flops 8 | bytes 64 | tf_op jit(solution)/shard_map/psum | solution.py:192
  178.4 2.9 %constant_dynamic-slice_fusion.6 = (f32[3,8,64,16]{3,2,1,0:T(8,128)}, f32[3,8,64,16]{3,2,1,0:T(8,128)}) fusion(f32[3,8,64,128]{3,2,1,0:T(8,128)} %copy-done.6, s32[]{:T(128)S(6)} %select_n.23, f32[3,8,64,128]{3,2,1,0:T(8,128)S(1)} %slice.1021), kind=kLoop, calls=%fused_computation.260 | loop fusion | bytes 393220 | tf_op jit(solution)/shard_map/dynamic_slice | solution.py:110
  181.4 2.8 %collective-permute-start.16 = (f32[4,3,4,64]{3,2,1,0:T(4,128)S(1)}, f32[4,3,4,64]{3,2,1,0:T(4,128)S(1)}, u32[]{:S(2)}, u32[]{:S(2)}) collective-permute-start(f32[4,3,4,64]{3,2,1,0:T(4,128)S(1)} %get-tuple-element.171), channel_id=1, source_target_pairs={{0,4},{4,8},{8,12},{12,16},{16,20},{20,24},{24,28},{1,5},{5,9},{9,... | collective-permute-start | bytes 36872 | tf_op jit(solution)/shard_map/ppermute | solution.py:22
  184.2 1.3 collective-permute-start.17
  185.6 1.5 subtract_bitcast_fusion.20
  187.0 1.1 constant_dynamic-slice_fusion.5
  189.6 5.9 %collective-permute-start.18 = (f32[4,3,16,4]{3,2,1,0:T(8,128)}, f32[4,3,16,4]{3,2,1,0:T(8,128)}, u32[]{:S(2)}, u32[]{:S(2)}) collective-permute-start(f32[4,3,16,4]{3,2,1,0:T(8,128)} %get-tuple-element.169), channel_id=1, source_target_pairs={{0,1},{1,2},{2,3},{4,5},{5,6},{6,7},{8,9},{9,10},{10,11},{12,13},{... | collective-permute-start | bytes 9224 | tf_op jit(solution)/shard_map/ppermute | solution.py:22
  195.5 2.2 collective-permute-start.19
  197.6 1.2 constant_dynamic-slice_fusion.4
  198.8 2.2 mul.702
  201.0 2.2 mul.698
  203.2 2.2 mul.706
  205.3 2.2 mul.710
  207.5 1.2 pad_maximum_fusion.14
  208.7 1.9 fusion.1
  213.1 1.3 copy-done.1
  214.6 1.3 fusion.14
  219.3 2.0 fusion.18
  222.8 1.1 fusion.20
  223.9 1.1 slice_bitcast_fusion.49
  225.0 1.2 slice_bitcast_fusion.2
  226.2 1.2 constant_dynamic-slice_fusion.3
  227.4 1.5 mul.728
  228.9 1.2 constant_dynamic-slice_fusion.2
  230.1 1.5 mul.737
  231.6 2.1 subtract_bitcast_fusion.2
  233.8 1.5 fusion.73
  239.9 3.8 %collective-permute-start.20 = (f32[2,64]{1,0:T(2,128)S(1)}, f32[2,64]{1,0:T(2,128)S(1)}, u32[]{:S(2)}, u32[]{:S(2)}) collective-permute-start(f32[2,64]{1,0:T(2,128)S(1)} %get-tuple-element.179), channel_id=1, source_target_pairs={{0,4},{4,8},{8,12},{12,16},{16,20},{20,24},{24,28},{1,5},{5,9},{9,... | collective-permute-start | bytes 1544 | tf_op jit(solution)/shard_map/ppermute | solution.py:22
  243.7 1.3 collective-permute-start.21
  245.0 3.0 %collective-permute-done.21 = f32[2,64]{1,0:T(2,128)S(1)} collective-permute-done((f32[2,64]{1,0:T(2,128)S(1)}, f32[2,64]{1,0:T(2,128)S(1)}, u32[]{:S(2)}, u32[]{:S(2)}) %collective-permute-start.21) | collective-permute-done | bytes 544 | tf_op jit(solution)/shard_map/ppermute | solution.py:25
  248.1 5.1 %collective-permute-start.22 = (f32[12,2]{1,0:T(8,128)S(1)}, f32[12,2]{1,0:T(8,128)S(1)}, u32[]{:S(2)}, u32[]{:S(2)}) collective-permute-start(f32[12,2]{1,0:T(8,128)S(1)} %get-tuple-element.173), channel_id=1, source_target_pairs={{0,1},{1,2},{2,3},{4,5},{5,6},{6,7},{8,9},{9,10},{10,11},{12,13},{... | collective-permute-start | bytes 296 | tf_op jit(solution)/shard_map/ppermute | solution.py:22
  253.2 1.9 collective-permute-start.23
  255.1 3.0 %collective-permute-done.23 = f32[12,2]{1,0:T(8,128)S(1)} collective-permute-done((f32[12,2]{1,0:T(8,128)S(1)}, f32[12,2]{1,0:T(8,128)S(1)}, u32[]{:S(2)}, u32[]{:S(2)}) %collective-permute-start.23) | collective-permute-done | bytes 128 | tf_op jit(solution)/shard_map/ppermute | solution.py:25
  (291 shorter events, 37.9 us)
Async XLA Ops:
  0.6 7.2 %copy-start.20 = (f32[3,8,64,128]{3,2,1,0:T(8,128)S(1)}, f32[3,8,64,128]{3,2,1,0:T(8,128)}, u32[]{:S(2)}) copy-start(f32[3,8,64,128]{3,2,1,0:T(8,128)} %param.13) | copy-start | bytes 2359300
  1.4 21.3 %collective-permute-start = (f32[2,64]{1,0:T(2,128)S(1)}, f32[2,64]{1,0:T(2,128)S(1)}, u32[]{:S(2)}, u32[]{:S(2)}) collective-permute-start(f32[2,64]{1,0:T(2,128)S(1)} %get-tuple-element.181), channel_id=1, source_target_pairs={{0,4},{4,8},{8,12},{12,16},{16,20},{20,24},{24,28},{1,5},{5,9},{9,... | collective-permute-start | bytes 1544 | tf_op jit(solution)/shard_map/ppermute | solution.py:22
  5.4 17.3 %collective-permute-start.1 = (f32[2,64]{1,0:T(2,128)S(1)}, f32[2,64]{1,0:T(2,128)S(1)}, u32[]{:S(2)}, u32[]{:S(2)}) collective-permute-start(f32[2,64]{1,0:T(2,128)S(1)} %get-tuple-element.182), channel_id=1, source_target_pairs={{4,0},{8,4},{12,8},{16,12},{20,16},{24,20},{28,24},{5,1},{9,5},{13... | collective-permute-start | bytes 1544 | tf_op jit(solution)/shard_map/ppermute | solution.py:25
  7.9 7.5 %copy-start.21 = (f32[3,8,64,128]{3,2,1,0:T(8,128)S(1)}, f32[3,8,64,128]{3,2,1,0:T(8,128)}, u32[]{:S(2)}) copy-start(f32[3,8,64,128]{3,2,1,0:T(8,128)} %param.10) | copy-start | bytes 2359300
  8.0 7.6 %copy-start.22 = (f32[3,8,64,128]{3,2,1,0:T(8,128)S(1)}, f32[3,8,64,128]{3,2,1,0:T(8,128)}, u32[]{:S(2)}) copy-start(f32[3,8,64,128]{3,2,1,0:T(8,128)} %param.11) | copy-start | bytes 2359300
  9.3 96.5 %collective-permute-start.12 = (f32[6,4,64,128]{3,2,1,0:T(8,128)}, f32[6,4,64,128]{3,2,1,0:T(8,128)}, u32[]{:S(2)}, u32[]{:S(2)}) collective-permute-start(f32[6,4,64,128]{3,2,1,0:T(8,128)} %get-tuple-element.159), channel_id=1, source_target_pairs={{0,4},{4,8},{8,12},{12,16},{16,20},{20,24},{24,28},{1,5},{5,9},{9,... | collective-permute-start | bytes 2359304 | tf_op jit(solution)/shard_map/ppermute | solution.py:22
  14.1 91.6 %collective-permute-start.13 = (f32[6,4,64,128]{3,2,1,0:T(8,128)}, f32[6,4,64,128]{3,2,1,0:T(8,128)}, u32[]{:S(2)}, u32[]{:S(2)}) collective-permute-start(f32[6,4,64,128]{3,2,1,0:T(8,128)} %get-tuple-element.160), channel_id=1, source_target_pairs={{4,0},{8,4},{12,8},{16,12},{20,16},{24,20},{28,24},{5,1},{9,5},{13... | collective-permute-start | bytes 2359304 | tf_op jit(solution)/shard_map/ppermute | solution.py:25
  15.6 82.3 %copy-start.3 = (f32[6,8,64,128]{3,2,1,0:T(8,128)}, f32[6,8,64,128]{3,2,1,0:T(8,128)S(1)}, u32[]{:S(2)}) copy-start(f32[6,8,64,128]{3,2,1,0:T(8,128)S(1)} %constant_dynamic-update-slice_fusion) | copy-start | bytes 4718596
  15.6 6.8 %copy-start.58 = (s32[1,8]{1,0:T(1,128)S(1)}, s32[1,8]{1,0:T(1,128)}, u32[]{:S(2)}) copy-start(s32[1,8]{1,0:T(1,128)} %param.16) | copy-start | bytes 100
  15.6 7.1 %copy-start.36 = (f32[8,64]{1,0:T(8,128)S(1)}, f32[8,64]{1,0:T(8,128)}, u32[]{:S(2)}) copy-start(f32[8,64]{1,0:T(8,128)} %param.15) | copy-start | bytes 6148
  15.6 23.5 %copy-start.34 = (s32[8]{0:T(128)S(1)}, s32[8]{0:T(128)}, u32[]{:S(2)}) copy-start(s32[8]{0:T(128)} %param.18) | copy-start | bytes 100
  16.9 79.1 %collective-permute-start.4 = (f32[6,4,64,128]{3,2,1,0:T(8,128)}, f32[6,4,64,128]{3,2,1,0:T(8,128)}, u32[]{:S(2)}, u32[]{:S(2)}) collective-permute-start(f32[6,4,64,128]{3,2,1,0:T(8,128)} %get-tuple-element.157), channel_id=1, source_target_pairs={{0,4},{4,8},{8,12},{12,16},{16,20},{20,24},{24,28},{1,5},{5,9},{9,... | collective-permute-start | bytes 2359304 | tf_op jit(solution)/shard_map/ppermute | solution.py:22
  22.7 13.2 %copy-start.56 = (f32[64]{0:T(128)}, f32[64]{0:T(128)S(1)}, u32[]{:S(2)}) copy-start(f32[64]{0:T(128)S(1)} %mul.309) | copy-start | bytes 772
  22.8 7.0 %collective-permute-start.2 = (f32[12,2]{1,0:T(8,128)S(1)}, f32[12,2]{1,0:T(8,128)S(1)}, u32[]{:S(2)}, u32[]{:S(2)}) collective-permute-start(f32[12,2]{1,0:T(8,128)S(1)} %get-tuple-element.177), channel_id=1, source_target_pairs={{0,1},{1,2},{2,3},{4,5},{5,6},{6,7},{8,9},{9,10},{10,11},{12,13},{... | collective-permute-start | bytes 296 | tf_op jit(solution)/shard_map/ppermute | solution.py:22
  27.9 5.4 %collective-permute-start.3 = (f32[12,2]{1,0:T(8,128)S(1)}, f32[12,2]{1,0:T(8,128)S(1)}, u32[]{:S(2)}, u32[]{:S(2)}) collective-permute-start(f32[12,2]{1,0:T(8,128)S(1)} %get-tuple-element.178), channel_id=1, source_target_pairs={{1,0},{2,1},{3,2},{5,4},{6,5},{7,6},{9,8},{10,9},{11,10},{13,12},{... | collective-permute-start | bytes 296 | tf_op jit(solution)/shard_map/ppermute | solution.py:25
  29.9 68.1 %collective-permute-start.5 = (f32[6,4,64,128]{3,2,1,0:T(8,128)}, f32[6,4,64,128]{3,2,1,0:T(8,128)}, u32[]{:S(2)}, u32[]{:S(2)}) collective-permute-start(f32[6,4,64,128]{3,2,1,0:T(8,128)} %get-tuple-element.158), channel_id=1, source_target_pairs={{4,0},{8,4},{12,8},{16,12},{20,16},{24,20},{28,24},{5,1},{9,5},{13... | collective-permute-start | bytes 2359304 | tf_op jit(solution)/shard_map/ppermute | solution.py:25
  35.9 46.5 %collective-permute-start.8 = (f32[4,64,128]{2,1,0:T(8,128)S(1)}, f32[4,64,128]{2,1,0:T(8,128)S(1)}, u32[]{:S(2)}, u32[]{:S(2)}) collective-permute-start(f32[4,64,128]{2,1,0:T(8,128)S(1)} %get-tuple-element.163), channel_id=1, source_target_pairs={{0,4},{4,8},{8,12},{12,16},{16,20},{20,24},{24,28},{1,5},{5,9},{9,... | collective-permute-start | bytes 393224 | tf_op jit(solution)/shard_map/ppermute | solution.py:22
  39.7 94.6 %copy-start.40 = (f32[8]{0:T(128)}, f32[8]{0:T(128)S(1)}, u32[]{:S(2)}) copy-start(f32[8]{0:T(128)S(1)} %get-tuple-element.183) | copy-start | bytes 100
  82.4 6.9 %collective-permute-start.9 = (f32[4,64,128]{2,1,0:T(8,128)}, f32[4,64,128]{2,1,0:T(8,128)}, u32[]{:S(2)}, u32[]{:S(2)}) collective-permute-start(f32[4,64,128]{2,1,0:T(8,128)} %get-tuple-element.164), channel_id=1, source_target_pairs={{4,0},{8,4},{12,8},{16,12},{20,16},{24,20},{28,24},{5,1},{9,5},{13... | collective-permute-start | bytes 393224 | tf_op jit(solution)/shard_map/ppermute | solution.py:25
  90.0 11.0 %collective-permute-start.10 = (f32[16,4,128]{2,1,0:T(4,128)S(1)}, f32[16,4,128]{2,1,0:T(4,128)S(1)}, u32[]{:S(2)}, u32[]{:S(2)}) collective-permute-start(f32[16,4,128]{2,1,0:T(4,128)S(1)} %get-tuple-element.161), channel_id=1, source_target_pairs={{0,1},{1,2},{2,3},{4,5},{5,6},{6,7},{8,9},{9,10},{10,11},{12,13},{... | collective-permute-start | bytes 98312 | tf_op jit(solution)/shard_map/ppermute | solution.py:22
  96.0 8.7 %collective-permute-start.11 = (f32[16,4,128]{2,1,0:T(4,128)S(1)}, f32[16,4,128]{2,1,0:T(4,128)S(1)}, u32[]{:S(2)}, u32[]{:S(2)}) collective-permute-start(f32[16,4,128]{2,1,0:T(4,128)S(1)} %get-tuple-element.162), channel_id=1, source_target_pairs={{1,0},{2,1},{3,2},{5,4},{6,5},{7,6},{9,8},{10,9},{11,10},{13,12},{... | collective-permute-start | bytes 98312 | tf_op jit(solution)/shard_map/ppermute | solution.py:25
  99.1 13.5 %collective-permute-start.7 = (f32[6,16,4,128]{3,1,2,0:T(8,128)S(1)}, f32[6,16,4,128]{3,1,2,0:T(8,128)S(1)}, u32[]{:S(2)}, u32[]{:S(2)}) collective-permute-start(f32[6,16,4,128]{3,1,2,0:T(8,128)S(1)} %copy.159), channel_id=1, source_target_pairs={{1,0},{2,1},{3,2},{5,4},{6,5},{7,6},{9,8},{10,9},{11,10},{13,12},{... | collective-permute-start | bytes 589832 | tf_op jit(solution)/shard_map/ppermute | solution.py:25
  101.1 11.7 %collective-permute-start.6 = (f32[6,16,4,128]{3,1,2,0:T(8,128)S(1)}, f32[6,16,4,128]{3,1,2,0:T(8,128)S(1)}, u32[]{:S(2)}, u32[]{:S(2)}) collective-permute-start(f32[6,16,4,128]{3,1,2,0:T(8,128)S(1)} %copy.158), channel_id=1, source_target_pairs={{0,1},{1,2},{2,3},{4,5},{5,6},{6,7},{8,9},{9,10},{10,11},{12,13},{... | collective-permute-start | bytes 589832 | tf_op jit(solution)/shard_map/ppermute | solution.py:22
  105.7 26.3 %copy-start.16 = (f32[8,64,128]{2,1,0:T(8,128)}, f32[8,64,128]{2,1,0:T(8,128)S(1)}, u32[]{:S(2)}) copy-start(f32[8,64,128]{2,1,0:T(8,128)S(1)} %slice.1078) | copy-start | bytes 786436
  105.7 7.1 %copy-start.4 = (f32[6,8,64,128]{3,2,1,0:T(8,128)S(1)}, f32[6,8,64,128]{3,2,1,0:T(8,128)}, u32[]{:S(2)}) copy-start(f32[6,8,64,128]{3,2,1,0:T(8,128)} %copy-done.3) | copy-start | bytes 4718596
  107.1 16.7 %collective-permute-start.15 = (f32[6,16,4,128]{3,1,2,0:T(8,128)S(1)}, f32[6,16,4,128]{3,1,2,0:T(8,128)S(1)}, u32[]{:S(2)}, u32[]{:S(2)}) collective-permute-start(f32[6,16,4,128]{3,1,2,0:T(8,128)S(1)} %copy.163), channel_id=1, source_target_pairs={{1,0},{2,1},{3,2},{5,4},{6,5},{7,6},{9,8},{10,9},{11,10},{13,12},{... | collective-permute-start | bytes 589832 | tf_op jit(solution)/shard_map/ppermute | solution.py:25
  109.0 14.9 %collective-permute-start.14 = (f32[6,16,4,128]{3,1,2,0:T(8,128)S(1)}, f32[6,16,4,128]{3,1,2,0:T(8,128)S(1)}, u32[]{:S(2)}, u32[]{:S(2)}) collective-permute-start(f32[6,16,4,128]{3,1,2,0:T(8,128)S(1)} %copy.162), channel_id=1, source_target_pairs={{0,1},{1,2},{2,3},{4,5},{5,6},{6,7},{8,9},{9,10},{10,11},{12,13},{... | collective-permute-start | bytes 589832 | tf_op jit(solution)/shard_map/ppermute | solution.py:22
  120.0 13.4 %copy-start.6 = (f32[3,8,64,128]{3,2,1,0:T(8,128)}, f32[3,8,64,128]{3,2,1,0:T(8,128)S(1)}, u32[]{:S(2)}) copy-start(f32[3,8,64,128]{3,2,1,0:T(8,128)S(1)} %slice.1040) | copy-start | bytes 2359300
  132.3 2.9 %copy-start.7 = (f32[3,8,64,128]{3,2,1,0:T(8,128)}, f32[3,8,64,128]{3,2,1,0:T(8,128)S(1)}, u32[]{:S(2)}) copy-start(f32[3,8,64,128]{3,2,1,0:T(8,128)S(1)} %get-tuple-element.92) | copy-start | bytes 2359300
  132.3 2.9 %copy-start.9 = (f32[3,8,64,128]{3,2,1,0:T(8,128)}, f32[3,8,64,128]{3,2,1,0:T(8,128)S(1)}, u32[]{:S(2)}) copy-start(f32[3,8,64,128]{3,2,1,0:T(8,128)S(1)} %get-tuple-element.91) | copy-start | bytes 2359300
  132.3 2.1 copy-start.31
  132.3 2.1 copy-start.42
  132.3 2.1 copy-start.44
  132.3 2.1 copy-start.46
  132.3 2.1 copy-start.48
  132.4 2.1 copy-start.50
  132.4 2.1 copy-start.52
  132.4 2.1 copy-start.54
  176.1 63.1 %copy-start.35 = (f32[8]{0:T(128)}, f32[8]{0:T(128)S(1)}, u32[]{:S(2)}) copy-start(f32[8]{0:T(128)S(1)} %broadcast_divide_fusion) | copy-start | bytes 100
  178.3 7.2 %copy-start.11 = (f32[16,72,128]{2,1,0:T(8,128)S(1)}, f32[16,72,128]{2,1,0:T(8,128)}, u32[]{:S(2)}) copy-start(f32[16,72,128]{2,1,0:T(8,128)} %get-tuple-element.153) | copy-start | bytes 1769476
  178.3 7.2 %copy-start.14 = (f32[16,72,128]{2,1,0:T(8,128)S(1)}, f32[16,72,128]{2,1,0:T(8,128)}, u32[]{:S(2)}) copy-start(f32[16,72,128]{2,1,0:T(8,128)} %get-tuple-element.152) | copy-start | bytes 1769476
  178.3 7.2 %copy-start.15 = (f32[16,72,128]{2,1,0:T(8,128)S(1)}, f32[16,72,128]{2,1,0:T(8,128)}, u32[]{:S(2)}) copy-start(f32[16,72,128]{2,1,0:T(8,128)} %get-tuple-element.154) | copy-start | bytes 1769476
  178.3 7.2 %copy-start.18 = (f32[15,72,128]{2,1,0:T(8,128)S(1)}, f32[15,72,128]{2,1,0:T(8,128)}, u32[]{:S(2)}) copy-start(f32[15,72,128]{2,1,0:T(8,128)} %get-tuple-element.155) | copy-start | bytes 1658884
  178.3 7.2 %copy-start.19 = (f32[15,72,128]{2,1,0:T(8,128)S(1)}, f32[15,72,128]{2,1,0:T(8,128)}, u32[]{:S(2)}) copy-start(f32[15,72,128]{2,1,0:T(8,128)} %get-tuple-element.156) | copy-start | bytes 1658884
  181.3 7.5 %copy-start.27 = (f32[1,3,8,64]{3,2,1,0:T(8,128)}, f32[1,3,8,64]{3,2,1,0:T(8,128)S(1)}, u32[]{:S(2)}) copy-start(f32[1,3,8,64]{3,2,1,0:T(8,128)S(1)} %subtract_bitcast_fusion.48) | copy-start | bytes 18436
  181.3 7.5 %copy-start.28 = (f32[1,3,8,64]{3,2,1,0:T(8,128)}, f32[1,3,8,64]{3,2,1,0:T(8,128)S(1)}, u32[]{:S(2)}) copy-start(f32[1,3,8,64]{3,2,1,0:T(8,128)S(1)} %subtract_bitcast_fusion.49) | copy-start | bytes 18436
  181.3 7.4 %copy-start.29 = (f32[1,3,8,64]{3,2,1,0:T(8,128)}, f32[1,3,8,64]{3,2,1,0:T(8,128)S(1)}, u32[]{:S(2)}) copy-start(f32[1,3,8,64]{3,2,1,0:T(8,128)S(1)} %subtract_bitcast_fusion.51) | copy-start | bytes 18436
  181.3 7.4 %copy-start.30 = (f32[1,3,8,64]{3,2,1,0:T(8,128)}, f32[1,3,8,64]{3,2,1,0:T(8,128)S(1)}, u32[]{:S(2)}) copy-start(f32[1,3,8,64]{3,2,1,0:T(8,128)S(1)} %subtract_bitcast_fusion.50) | copy-start | bytes 18436
  181.4 6.8 %collective-permute-start.16 = (f32[4,3,4,64]{3,2,1,0:T(4,128)S(1)}, f32[4,3,4,64]{3,2,1,0:T(4,128)S(1)}, u32[]{:S(2)}, u32[]{:S(2)}) collective-permute-start(f32[4,3,4,64]{3,2,1,0:T(4,128)S(1)} %get-tuple-element.171), channel_id=1, source_target_pairs={{0,4},{4,8},{8,12},{12,16},{16,20},{20,24},{24,28},{1,5},{5,9},{9,... | collective-permute-start | bytes 36872 | tf_op jit(solution)/shard_map/ppermute | solution.py:22
  184.2 4.6 %collective-permute-start.17 = (f32[4,3,4,64]{3,2,1,0:T(4,128)S(1)}, f32[4,3,4,64]{3,2,1,0:T(4,128)S(1)}, u32[]{:S(2)}, u32[]{:S(2)}) collective-permute-start(f32[4,3,4,64]{3,2,1,0:T(4,128)S(1)} %get-tuple-element.172), channel_id=1, source_target_pairs={{4,0},{8,4},{12,8},{16,12},{20,16},{24,20},{28,24},{5,1},{9,5},{13... | collective-permute-start | bytes 36872 | tf_op jit(solution)/shard_map/ppermute | solution.py:25
  187.0 10.6 %copy-start.8 = (f32[3,8,64,128]{3,2,1,0:T(8,128)S(1)}, f32[3,8,64,128]{3,2,1,0:T(8,128)}, u32[]{:S(2)}) copy-start(f32[3,8,64,128]{3,2,1,0:T(8,128)} %copy-done.7) | copy-start | bytes 2359300
  188.2 10.6 %copy-start.32 = (f32[4,3,4,64]{3,2,1,0:T(4,128)}, f32[4,3,4,64]{3,2,1,0:T(4,128)S(1)}, u32[]{:S(2)}) copy-start(f32[4,3,4,64]{3,2,1,0:T(4,128)S(1)} %collective-permute-done.16) | copy-start | bytes 36868
  188.8 10.0 %copy-start.33 = (f32[4,3,4,64]{3,2,1,0:T(4,128)}, f32[4,3,4,64]{3,2,1,0:T(4,128)S(1)}, u32[]{:S(2)}) copy-start(f32[4,3,4,64]{3,2,1,0:T(4,128)S(1)} %collective-permute-done.17) | copy-start | bytes 36868
  189.6 17.9 %collective-permute-start.18 = (f32[4,3,16,4]{3,2,1,0:T(8,128)}, f32[4,3,16,4]{3,2,1,0:T(8,128)}, u32[]{:S(2)}, u32[]{:S(2)}) collective-permute-start(f32[4,3,16,4]{3,2,1,0:T(8,128)} %get-tuple-element.169), channel_id=1, source_target_pairs={{0,1},{1,2},{2,3},{4,5},{5,6},{6,7},{8,9},{9,10},{10,11},{12,13},{... | collective-permute-start | bytes 9224 | tf_op jit(solution)/shard_map/ppermute | solution.py:22
  195.5 12.1 %collective-permute-start.19 = (f32[4,3,16,4]{3,2,1,0:T(8,128)}, f32[4,3,16,4]{3,2,1,0:T(8,128)}, u32[]{:S(2)}, u32[]{:S(2)}) collective-permute-start(f32[4,3,16,4]{3,2,1,0:T(8,128)} %get-tuple-element.170), channel_id=1, source_target_pairs={{1,0},{2,1},{3,2},{5,4},{6,5},{7,6},{9,8},{10,9},{11,10},{13,12},{... | collective-permute-start | bytes 9224 | tf_op jit(solution)/shard_map/ppermute | solution.py:25
  201.0 7.7 %copy-start.38 = (f32[128]{0:T(128)S(1)}, f32[128]{0:T(128)}, u32[]{:S(2)}) copy-start(f32[128]{0:T(128)} %compare_convert_fusion) | copy-start | bytes 1540
  212.5 2.1 copy-start.5
  226.1 2.8 %copy-start.12 = (f32[3,8,64,128]{3,2,1,0:T(8,128)S(1)}, f32[3,8,64,128]{3,2,1,0:T(8,128)}, u32[]{:S(2)}) copy-start(f32[3,8,64,128]{3,2,1,0:T(8,128)} %slice.1127) | copy-start | bytes 2359300
  231.6 2.1 copy-start.17
  231.6 2.1 copy-start.39
  239.9 5.2 %collective-permute-start.20 = (f32[2,64]{1,0:T(2,128)S(1)}, f32[2,64]{1,0:T(2,128)S(1)}, u32[]{:S(2)}, u32[]{:S(2)}) collective-permute-start(f32[2,64]{1,0:T(2,128)S(1)} %get-tuple-element.179), channel_id=1, source_target_pairs={{0,4},{4,8},{8,12},{12,16},{16,20},{20,24},{24,28},{1,5},{5,9},{9,... | collective-permute-start | bytes 1544 | tf_op jit(solution)/shard_map/ppermute | solution.py:22
  243.7 4.3 %collective-permute-start.21 = (f32[2,64]{1,0:T(2,128)S(1)}, f32[2,64]{1,0:T(2,128)S(1)}, u32[]{:S(2)}, u32[]{:S(2)}) collective-permute-start(f32[2,64]{1,0:T(2,128)S(1)} %get-tuple-element.180), channel_id=1, source_target_pairs={{4,0},{8,4},{12,8},{16,12},{20,16},{24,20},{28,24},{5,1},{9,5},{13... | collective-permute-start | bytes 1544 | tf_op jit(solution)/shard_map/ppermute | solution.py:25
  248.1 7.0 %collective-permute-start.22 = (f32[12,2]{1,0:T(8,128)S(1)}, f32[12,2]{1,0:T(8,128)S(1)}, u32[]{:S(2)}, u32[]{:S(2)}) collective-permute-start(f32[12,2]{1,0:T(8,128)S(1)} %get-tuple-element.173), channel_id=1, source_target_pairs={{0,1},{1,2},{2,3},{4,5},{5,6},{6,7},{8,9},{9,10},{10,11},{12,13},{... | collective-permute-start | bytes 296 | tf_op jit(solution)/shard_map/ppermute | solution.py:22
  253.2 5.0 %collective-permute-start.23 = (f32[12,2]{1,0:T(8,128)S(1)}, f32[12,2]{1,0:T(8,128)S(1)}, u32[]{:S(2)}, u32[]{:S(2)}) collective-permute-start(f32[12,2]{1,0:T(8,128)S(1)} %get-tuple-element.174), channel_id=1, source_target_pairs={{1,0},{2,1},{3,2},{5,4},{6,5},{7,6},{9,8},{10,9},{11,10},{13,12},{... | collective-permute-start | bytes 296 | tf_op jit(solution)/shard_map/ppermute | solution.py:25
  (19 other events, 24.4 us)
where the time goes:
time: 260 us; the launch traced here: 259 us
  starting transfers between devices  72.3 us (28%)
  waiting for transfers between devices  55.3 us (21%)
  local copies, waits for them, and re-layouts  45.7 us (18%)
  other arithmetic  40.1 us (15%)
  blocking collectives  39.6 us (15%)
  between operations  3.24 us (1%)
  matrix products  2.72 us (1%)
    ppermute x12, starting transfers between devices, with_halo(): lax.ppermute(lax.slice_in_dim(block, block.shape[dim] - width, None, axis...  52.8 us
    ppermute x12, waiting for transfers between devices, with_halo(): lax.ppermute(lax.slice_in_dim(block, block.shape[dim] - width, None, axis...  42.7 us
    psum x1, blocking collectives, body(): loss_sums = lax.psum(local_sums, ('gx', 'gy'))  39.6 us
    ppermute x12, starting transfers between devices, with_halo(): lax.ppermute(lax.slice_in_dim(block, 0, width, axis=dim), axis, backward)  19.5 us
    mul x8, local copies, waits for them, and re-layouts, add_transforms(): slab_re = slab_re + cosines[:, None, None, None] * slab_cells[None]  12.6 us
    ppermute x12, waiting for transfers between devices, with_halo(): lax.ppermute(lax.slice_in_dim(block, 0, width, axis=dim), axis, backward)  12.6 us
    dynamic_slice x7, local copies, waits for them, and re-layouts, add_transforms(): lax.dynamic_slice_in_dim(e_own, z_floor, DZ, 3)  8.09 us
    another operation x8, other arithmetic, curl_behind(): return jnp.stack([curl_x, curl_y, curl_z])  7.65 us
  transfers between devices with their start and end apart: 24, of which 6 were waited for; matrix products, arithmetic and copies ran while one was open for 14% of the time, Pallas kernels for 0%

commit v1 on v0

v1 whole, which is shorter than its diff:
```python
import functools

import jax
import jax.numpy as jnp
from jax import lax
from jax.experimental import pallas as pl
from jax.experimental.pallas import tpu as pltpu
from jax.sharding import PartitionSpec as P

STEPS = 4
DZ = 16
TILE = 8
LANES = 128

courant = 0.5
sharpness = 4.0
contrast = 10.0
threshold = 0.5

MESH = pl.DeviceIdType.MESH
F32 = jnp.float32


def when(cond):
    return pl.when(cond)


def kernel(
    nx, ny, nf, rx, ry, nz,
    floor_ref, tiles_ref, cos_ref, sin_ref, pair_ref, design_ref, target_ref,
    e_in, h_in, ae_in, ah_in, eps_in,
    grad_ref, weights_ref, e_out, ae_out,
    es, hs, eps, scale, hx, hy, plane, planes_t, source, sens, mis,
    fx, fy, part_x, part_y, gbuf,
    in_sem, out_sem, ssem, rsem, fsend, frecv, psend, precv,
):
    gx = lax.axis_index("gx")
    gy = lax.axis_index("gy")

    loads = [
        pltpu.make_async_copy(e_in, es.at[0, 0], in_sem.at[0]),
        pltpu.make_async_copy(ae_in, es.at[1, 0], in_sem.at[1]),
        pltpu.make_async_copy(h_in, hs.at[0, 0], in_sem.at[2]),
        pltpu.make_async_copy(ah_in, hs.at[1, 0], in_sem.at[3]),
        pltpu.make_async_copy(eps_in, eps, in_sem.at[4]),
    ]
    for load in loads:
        load.start()

    barrier = pltpu.get_barrier_semaphore()
    hx[...] = jnp.zeros_like(hx)
    hy[...] = jnp.zeros_like(hy)
    fx[...] = jnp.zeros_like(fx)
    fy[...] = jnp.zeros_like(fy)
    for k in range(1, nx):
        pl.semaphore_signal(barrier, inc=1, device_id=(lax.rem(gx + k, nx), gy), device_id_type=MESH)
    for k in range(1, ny):
        pl.semaphore_signal(barrier, inc=1, device_id=(gx, lax.rem(gy + k, ny)), device_id_type=MESH)

    row = lax.broadcasted_iota(jnp.int32, (ry, nz), 0)
    lane = lax.broadcasted_iota(jnp.int32, (ry, nz), 1)
    z0 = floor_ref[0]
    at_monitor = lane == z0 + DZ
    in_slab = (lane >= z0) & (lane < z0 + DZ)

    def copies(run, t, kind):
        slot = run * 2 * STEPS + 2 * t + kind
        if kind == 0:
            src, layer, rows, dx, dy = es.at[run, t], 0, pl.ds(0, 8), gx - 1, gy - 1
        else:
            src, layer, rows, dx, dy = hs.at[run, t + 1], rx - 1, pl.ds(ry - 8, 8), gx + 1, gy + 1
        in_x = pltpu.make_async_remote_copy(
            src.at[pl.ds(1, 2), layer], hx.at[slot], ssem.at[slot, 0], rsem.at[slot, 0],
            device_id=(dx, gy), device_id_type=MESH)
        in_y = [
            pltpu.make_async_remote_copy(
                src.at[2 * j, :, rows], hy.at[slot, j], ssem.at[slot, 1 + j], rsem.at[slot, 1 + j],
                device_id=(gx, dy), device_id_type=MESH)
            for j in range(2)
        ]
        return in_x, in_y

    low = (gx > 0, gy > 0)
    high = (gx < nx - 1, gy < ny - 1)

    def send_x(run, t, kind):
        @when((low, high)[kind][0])
        def _():
            copies(run, t, kind)[0].start()

    def send_y(run, t, kind):
        @when((low, high)[kind][1])
        def _():
            for copy in copies(run, t, kind)[1]:
                copy.start()

    def receive(run, t, kind):
        @when((high, low)[kind][0])
        def _():
            copies(run, t, kind)[0].wait_recv()

        @when((high, low)[kind][1])
        def _():
            for copy in copies(run, t, kind)[1]:
                copy.wait_recv()

    def finish(run, t, kind):
        @when((low, high)[kind][0])
        def _():
            copies(run, t, kind)[0].wait_send()

        @when((low, high)[kind][1])
        def _():
            for copy in copies(run, t, kind)[1]:
                copy.wait_send()

    def next_y(v, face):
        return jnp.where(row == ry - 1, face, pltpu.roll(v, ry - 1, 0))

    def next_z(v):
        return jnp.where(lane == nz - 1, 0.0, pltpu.roll(v, nz - 1, 1))

    def last_y(v, face):
        return jnp.where(row == 0, face, pltpu.roll(v, 1, 0))

    def last_z(v):
        return jnp.where(lane == 0, 0.0, pltpu.roll(v, 1, 1))

    def h_layer(run, t, i, ey_next, ez_next):
        slot = run * 2 * STEPS + 2 * t
        ex, ey, ez = (es[run, t, c, i] for c in range(3))
        face_x, face_z = hy[slot, 0, i, 0:1, :], hy[slot, 1, i, 0:1, :]
        hs[run, t + 1, 0, i] = hs[run, t, 0, i] - courant * (
            (next_y(ez, face_z) - ez) - (next_z(ey) - ey))
        hs[run, t + 1, 1, i] = hs[run, t, 1, i] - courant * ((next_z(ex) - ex) - (ez_next - ez))
        hs[run, t + 1, 2, i] = hs[run, t, 2, i] - courant * (
            (ey_next - ey) - (next_y(ex, face_x) - ex))

    def h_step(run, t):
        slot = run * 2 * STEPS + 2 * t
        receive(run, t, 0)
        h_layer(run, t, rx - 1, hx[slot, 0], hx[slot, 1])
        send_x(run, t, 1)

        def inner(i, carry):
            h_layer(run, t, i, es[run, t, 1, i + 1], es[run, t, 2, i + 1])
            return carry

        lax.fori_loop(0, rx - 1, inner, 0)
        send_y(run, t, 1)

    def column(t, c, i):
        return lane == (c * STEPS + t) * rx + i

    def e_layer(run, t, i, hy_last, hz_last, sourced):
        slot = run * 2 * STEPS + 2 * t + 1
        mx, my, mz = (hs[run, t + 1, c, i] for c in range(3))
        face_x, face_z = hy[slot, 0, i, 7:8, :], hy[slot, 1, i, 7:8, :]
        s = scale[i]
        new = [
            es[run, t, 0, i] + s * ((mz - last_y(mz, face_z)) - (my - last_z(my))),
            es[run, t, 1, i] + s * ((mx - last_z(mx)) - (mz - hz_last)),
            es[run, t, 2, i] + s * ((my - hy_last) - (mx - last_y(mx, face_x))),
        ]
        for c in range(3):
            if sourced:
                new[c] = new[c] + source_term(t, c, i)
            es[run, t + 1, c, i] = new[c]

    def source_term(t, c, i):
        value = jnp.sum(jnp.where(column(t, c, i), source[...], 0.0), axis=1, keepdims=True)
        return jnp.where(at_monitor, value, 0.0)

    def e_step(run, t, sourced, send):
        slot = run * 2 * STEPS + 2 * t + 1
        receive(run, t, 1)
        e_layer(run, t, 0, hx[slot, 0], hx[slot, 1], sourced)
        if send:
            send_x(run, t + 1, 0)

        def inner(i, carry):
            e_layer(run, t, i, hs[run, t + 1, 1, i - 1], hs[run, t + 1, 2, i - 1], sourced)
            return carry

        lax.fori_loop(1, rx, inner, 0)
        if send:
            send_y(run, t + 1, 0)

    def watch(t):
        def one(i, carry):
            total = plane[...]
            for c in range(3):
                value = jnp.sum(jnp.where(at_monitor, es[0, t + 1, c, i], 0.0), axis=1, keepdims=True)
                total = jnp.where(column(t, c, i), value, total)
            plane[...] = total
            return carry

        lax.fori_loop(0, rx, one, 0)

    def swaps(which):
        def along(buf, sems, send_to):
            return [
                pltpu.make_async_remote_copy(
                    buf.at[which, 1], buf.at[which, 2 - 2 * j], fsend.at[which, sems, j],
                    frecv.at[which, sems, j], device_id=send_to[j], device_id_type=MESH)
                for j in range(2)
            ]

        return (along(fx, 0, ((gx - 1, gy), (gx + 1, gy))), along(fy, 1, ((gx, gy - 1), (gx, gy + 1))))

    def swap_start(which, a):
        for j in range(2):
            @when((low, high)[j][a])
            def _():
                swaps(which)[a][j].start()

    def swap_wait(which, a):
        for j in range(2):
            @when((high, low)[j][a])
            def _():
                swaps(which)[a][j].wait_recv()

            @when((low, high)[j][a])
            def _():
                swaps(which)[a][j].wait_send()

    plane_lane = lax.broadcasted_iota(jnp.int32, (rx, LANES), 1)

    def filter_start(which, value):
        fx[which, 1] = value
        swap_start(which, 0)

    def filter_middle(which):
        swap_wait(which, 0)
        wide = jnp.concatenate([fx[which, 0], fx[which, 1], fx[which, 2]], 0)
        taps = [wide[rx - 2 + d: 2 * rx - 2 + d] for d in range(5)]
        fy[which, 1] = (taps[0] + 2.0 * taps[1] + 3.0 * taps[2] + 2.0 * taps[3] + taps[4]) / 9.0
        swap_start(which, 1)

    def filter_end(which):
        swap_wait(which, 1)
        below = pltpu.roll(fy[which, 0], LANES - ry, 1)
        above = pltpu.roll(fy[which, 2], ry, 1)
        wide = jnp.where(plane_lane < ry, fy[which, 1],
                         jnp.where(plane_lane < ry + 2, above,
                                   jnp.where(plane_lane >= LANES - 2, below, 0.0)))
        taps = [wide if d == 2 else pltpu.roll(wide, (2 - d) % LANES, 1) for d in range(5)]
        return (taps[0] + 2.0 * taps[1] + 3.0 * taps[2] + 2.0 * taps[3] + taps[4]) / 9.0

    pl.semaphore_wait(barrier, nx - 1 + ny - 1)
    gbuf[...] = jnp.zeros_like(gbuf)
    gbuf[0:rx, 0:ry] = design_ref[...]
    filter_start(0, gbuf[0:rx, :])
    plane[...] = jnp.zeros_like(plane)
    sens[...] = jnp.zeros_like(sens)
    for run in range(2):
        loads[run].wait()
        send_x(run, 0, 0)
        send_y(run, 0, 0)
    filter_middle(0)
    loads[2].wait()
    h_step(0, 0)
    loads[3].wait()
    h_step(1, 0)

    filtered = filter_end(0)
    tilted = jnp.tanh(sharpness * (filtered - threshold))
    offset_tanh = jnp.tanh(jnp.full((1, 1), sharpness * threshold, F32))
    projected = (offset_tanh + tilted) / (2.0 * offset_tanh)
    slope = sharpness * (1.0 - tilted * tilted) / (2.0 * offset_tanh)
    cells = jnp.zeros((rx, LANES), F32)
    for a in range(rx // TILE):
        for b in range(ry // TILE):
            x_of = lax.broadcasted_iota(jnp.int32, (rx, LANES), 0)
            here = (x_of // TILE == a) & (plane_lane // TILE == b)
            cells = jnp.where(here, tiles_ref[a, b].astype(F32), cells)
    gbuf[0:rx, :] = jnp.where(cells > 0.5, 1.0 + contrast * projected, -1.0)
    chosen = jnp.transpose(gbuf[...])[0:ry, :]
    slope = slope * cells
    loads[4].wait()
    for i in range(rx):
        value = jnp.sum(jnp.where(lane == i, chosen, 0.0), axis=1, keepdims=True)
        permittivity = jnp.where(in_slab & (value > 0.0), value, eps[i])
        scale[i] = courant / permittivity

    e_step(0, 0, False, True)
    e_step(1, 0, False, False)
    watch(0)

    def forward(t, carry):
        h_step(0, t)
        e_step(0, t, False, True)
        watch(t)
        return carry

    lax.fori_loop(1, STEPS - 1, forward, 0)
    h_step(0, STEPS - 1)
    e_step(0, STEPS - 1, False, False)
    watch(STEPS - 1)
    stores = [pltpu.make_async_copy(es.at[0, STEPS], e_out, out_sem.at[0]),
              pltpu.make_async_copy(es.at[1, STEPS], ae_out, out_sem.at[1])]
    stores[0].start()

    planes_t[...] = jnp.transpose(plane[...])

    def monitor(c, t):
        first = (c * STEPS + t) * rx
        return planes_t[first: first + rx, :]

    shown = [[monitor(c, t) for t in range(STEPS)] for c in range(3)]
    k_row = lax.broadcasted_iota(jnp.int32, (nf, LANES), 0)
    part = jnp.zeros((nf, LANES), F32)
    for k in range(nf):
        square = jnp.zeros((rx, ry), F32)
        for c in range(3):
            re = -target_ref[0, k, c]
            im = -target_ref[1, k, c]
            for t in range(STEPS):
                re = re + cos_ref[k, t] * shown[c][t]
                im = im - sin_ref[k, t] * shown[c][t]
            mis[0, k, c] = re
            mis[1, k, c] = im
            square = square + (re * re + im * im)
        total = jnp.sum(jnp.sum(square, axis=0, keepdims=True), axis=1, keepdims=True)
        part = jnp.where(k_row == k, total, part)

    def gathers(buf, axis):
        me, n = (gx, nx) if axis == 0 else (gy, ny)
        out = []
        for k in range(1, n):
            other = lax.rem(me + k, n)
            out.append(pltpu.make_async_remote_copy(
                buf.at[me], buf.at[me], psend.at[axis, k], precv.at[axis, k],
                device_id=(other, gy) if axis == 0 else (gx, other), device_id_type=MESH))
        return out

    def gather_sum(buf, axis, value):
        me, n = (gx, nx) if axis == 0 else (gy, ny)
        buf[me] = value
        for copy in gathers(buf, axis):
            copy.start()
        for copy in gathers(buf, axis):
            copy.wait()
        total = buf[0]
        for k in range(1, n):
            total = total + buf[k]
        return total

    loss_sums = gather_sum(part_y, 1, gather_sum(part_x, 0, part))
    losses = loss_sums / float(3 * rx * nx * ry * ny) + 1e-06
    squared = losses * losses
    weights = squared / jnp.sum(squared, axis=0, keepdims=True)
    weights_ref[...] = weights

    sources = [[jnp.zeros((rx, ry), F32) for _ in range(STEPS)] for _ in range(3)]
    for k in range(nf):
        w = weights[k:k + 1, 0:1]
        for c in range(3):
            re = w * mis[0, k, c]
            im = w * mis[1, k, c]
            for t in range(STEPS):
                sources[c][t] = sources[c][t] + (cos_ref[k, t] * re - sin_ref[k, t] * im)
    planes_t[...] = jnp.zeros_like(planes_t)
    for c in range(3):
        for t in range(STEPS):
            first = (c * STEPS + t) * rx
            planes_t[first: first + rx, :] = sources[c][t]
    source[...] = jnp.transpose(planes_t[...])
    mixed = jnp.sum(weights * pair_ref[...], axis=0, keepdims=True)

    def first_source(i, carry):
        for c in range(3):
            es[1, 1, c, i] = es[1, 1, c, i] + source_term(0, c, i)
        return carry

    lax.fori_loop(0, rx, first_source, 0)
    send_x(1, 1, 0)
    send_y(1, 1, 0)

    def correlate(s):
        lane_row = lax.broadcasted_iota(jnp.int32, (1, LANES), 1)
        factors = [
            jnp.sum(jnp.where(lane_row == t * STEPS + s, mixed, 0.0), axis=1, keepdims=True)
            for t in range(STEPS)
        ]

        def one(i, carry):
            total = sens[i]
            for c in range(3):
                mix = factors[0] * es[0, 1, c, i]
                for t in range(1, STEPS):
                    mix = mix + factors[t] * es[0, t + 1, c, i]
                total = total + mix * es[1, s + 1, c, i]
            sens[i] = total
            return carry

        lax.fori_loop(0, rx, one, 0)

    correlate(0)

    def adjoint(t, carry):
        h_step(1, t)
        e_step(1, t, True, True)
        correlate(t)
        return carry

    lax.fori_loop(1, STEPS - 1, adjoint, 0)
    h_step(1, STEPS - 1)
    e_step(1, STEPS - 1, True, False)
    stores[1].start()
    correlate(STEPS - 1)

    total = jnp.zeros((ry, nz), F32)
    for i in range(rx):
        value = jnp.sum(jnp.where(in_slab, sens[i], 0.0), axis=1, keepdims=True)
        total = jnp.where(lane == i, value, total)
    gbuf[...] = jnp.zeros_like(gbuf)
    gbuf[:, 0:ry] = jnp.transpose(total)
    density = gbuf[0:rx, :] / float(3 * DZ)
    filter_start(1, slope * density)
    filter_middle(1)
    grad_ref[...] = filter_end(1)[:, 0:ry]

    for run in range(2):
        for t in range(STEPS):
            for kind in range(2):
                finish(run, t, kind)
    for store in stores:
        store.wait()


def body(
    nx, ny, e_start, h_start, adj_e_start, adj_h_start, eps_background, design, design_tiles,
    design_floor, freq_index, target,
):
    rx, ry, nz = e_start.shape[1:]
    nf = freq_index.shape[0]
    angular = 0.3 + 0.04 * freq_index.astype(F32)
    times = jnp.arange(1, STEPS + 1, dtype=F32)
    phase = angular[:, None] * times[None, :]
    cosines, sines = jnp.cos(phase), jnp.sin(phase)
    pairs = cosines[:, :, None] * cosines[:, None, :] - sines[:, :, None] * sines[:, None, :]
    pairs = jnp.pad(pairs.reshape(nf, STEPS * STEPS), ((0, 0), (0, LANES - STEPS * STEPS)))
    smem = pl.BlockSpec(memory_space=pltpu.SMEM)
    vmem = pl.BlockSpec(memory_space=pltpu.VMEM)
    hbm = pl.BlockSpec(memory_space=pl.ANY)
    field = jax.ShapeDtypeStruct((3, rx, ry, nz), F32)
    slots = 4 * STEPS
    grad, weights, e_final, adj_e_final = pl.pallas_call(
        functools.partial(kernel, nx, ny, nf, rx, ry, nz),
        out_shape=(
            jax.ShapeDtypeStruct((rx, ry), F32),
            jax.ShapeDtypeStruct((nf, LANES), F32),
            field,
            field,
        ),
        in_specs=[smem, smem, smem, smem, vmem, vmem, vmem] + [hbm] * 5,
        out_specs=(vmem, vmem, hbm, hbm),
        scratch_shapes=[
            pltpu.VMEM((2, STEPS + 1, 3, rx, ry, nz), F32),
            pltpu.VMEM((2, STEPS + 1, 3, rx, ry, nz), F32),
            pltpu.VMEM((rx, ry, nz), F32),
            pltpu.VMEM((rx, ry, nz), F32),
            pltpu.VMEM((slots, 2, ry, nz), F32),
            pltpu.VMEM((slots, 2, rx, 8, nz), F32),
            pltpu.VMEM((ry, LANES), F32),
            pltpu.VMEM((LANES, ry), F32),
            pltpu.VMEM((ry, LANES), F32),
            pltpu.VMEM((rx, ry, nz), F32),
            pltpu.VMEM((2, nf, 3, rx, ry), F32),
            pltpu.VMEM((2, 3, rx, LANES), F32),
            pltpu.VMEM((2, 3, rx, LANES), F32),
            pltpu.VMEM((nx, nf, LANES), F32),
            pltpu.VMEM((ny, nf, LANES), F32),
            pltpu.VMEM((LANES, LANES), F32),
            pltpu.SemaphoreType.DMA((5,)),
            pltpu.SemaphoreType.DMA((2,)),
            pltpu.SemaphoreType.DMA((slots, 3)),
            pltpu.SemaphoreType.DMA((slots, 3)),
            pltpu.SemaphoreType.DMA((2, 2, 2)),
            pltpu.SemaphoreType.DMA((2, 2, 2)),
            pltpu.SemaphoreType.DMA((2, max(nx, ny))),
            pltpu.SemaphoreType.DMA((2, max(nx, ny))),
        ],
        compiler_params=pltpu.CompilerParams(
            collective_id=0, has_side_effects=True, vmem_limit_bytes=48 << 20
        ),
    )(
        design_floor, design_tiles, cosines, sines, pairs, design, target,
        e_start, h_start, adj_e_start, adj_h_start, eps_background,
    )
    return grad, weights[:, 0], e_final, adj_e_final


def solution(mesh):
    placed = (
        P(None, "gx", "gy", None),
        P(None, "gx", "gy", None),
        P(None, "gx", "gy", None),
        P(None, "gx", "gy", None),
        P("gx", "gy", None),
        P("gx", "gy"),
        P("gx", "gy"),
        P(),
        P(),
        P(None, None, None, "gx", "gy"),
    )
    return jax.shard_map(
        functools.partial(body, mesh.shape["gx"], mesh.shape["gy"]),
        mesh=mesh,
        in_specs=placed,
        out_specs=(P("gx", "gy"), P(), P(None, "gx", "gy", None), P(None, "gx", "gy", None)),
        check_vma=False,
    )
```

time: 260 us -> 88.8 us (0.34)
  Pallas kernels: 0 us -> 76.6 us
  starting transfers between devices: 72.3 us -> 0 us
  waiting for transfers between devices: 55.3 us -> 0 us
  other arithmetic: 40.1 us -> 0.13 us
  blocking collectives: 39.6 us -> 0 us
  local copies, waits for them, and re-layouts: 45.7 us -> 10.3 us
  matrix products: 2.72 us -> 0 us
    pallas_call x0 -> x1, Pallas kernels: none -> 76.6 us  [body(): pl.pallas_call(functools.partial(kernel, nx, ny, nf, rx, ry, nz), out_sha...]
    ppermute x24 -> x0, starting transfers between devices: 72.3 us -> none  [the longest x12 52.8 us: with_halo(): lax.ppermute(lax.slice_in_dim(block, block.shape[dim] - width, None, axis...]
    ppermute x24 -> x0, waiting for transfers between devices: 55.3 us -> none  [the longest x12 42.7 us: with_halo(): lax.ppermute(lax.slice_in_dim(block, block.shape[dim] - width, None, axis...]
    psum x1 -> x0, blocking collectives: 39.6 us -> none  [body(): loss_sums = lax.psum(local_sums, ('gx', 'gy'))]
    slice x66 -> x1, local copies, waits for them, and re-layouts: 13.7 us -> 0.63 us  [body(): return (grad, weights[:, 0], e_final, adj_e_final)]
    mul x11 -> x0, local copies, waits for them, and re-layouts: 12.8 us -> none  [the longest x8 12.6 us: add_transforms(): slab_re = slab_re + cosines[:, None, None, None] * slab_cells[None]]
    another operation x21 -> x0, other arithmetic: 10.2 us -> none  [the longest x8 7.65 us: curl_behind(): return jnp.stack([curl_x, curl_y, curl_z])]
    dynamic_slice x10 -> x0, local copies, waits for them, and re-layouts: 10 us -> none  [the longest x7 8.09 us: add_transforms(): lax.dynamic_slice_in_dim(e_own, z_floor, DZ, 3)]
  transfers between devices with their start and end apart: 24 -> 0, of which waited for: 6 -> 0; matrix products, arithmetic and copies ran while one was open for 14% -> 0% of each run, Pallas kernels for 0% -> 0%
where the time goes in v1:
time: 88.8 us; the launch traced here: 88.4 us
  Pallas kernels  76.6 us (86%)
  local copies, waits for them, and re-layouts  10.3 us (12%)
  between operations  1.34 us (2%)
    pallas_call x1, Pallas kernels, body(): pl.pallas_call(functools.partial(kernel, nx, ny, nf, rx, ry, nz), out_sha...  76.6 us
    unnamed x21, local copies, waits for them, and re-layouts  9.45 us

profile of v1, /device:TPU:1, one launch (start us, length us, event | category | flops | bytes accessed | tf_op | source)
XLA Modules:
  0.0 88.4 jit_solution(1619480793254883300)
XLA Ops:
  0.6 0.0 copy-start.8
  1.3 0.0 copy-done.8
  1.3 0.1 multiply_sine_fusion
  1.4 0.1 copy.21
  1.5 0.1 copy.19
  1.6 0.1 copy.23
  1.7 0.0 copy-start.6
  1.7 0.0 copy-start.7
  1.7 0.7 copy-done.6
  2.4 0.0 copy-done.7
  2.4 0.0 copy-start
  2.4 1.1 %copy-done = f32[3,8,64,128]{3,2,1,0:T(8,128)S(1)} copy-done((f32[3,8,64,128]{3,2,1,0:T(8,128)S(1)}, f32[3,8,64,128]{3,2,1,0:T(8,128)}, u32[]{:S(2)}) %copy-start) | copy-done | bytes 786456
  3.5 0.0 copy-start.1
  3.5 1.1 %copy-done.1 = f32[3,8,64,128]{3,2,1,0:T(8,128)S(1)} copy-done((f32[3,8,64,128]{3,2,1,0:T(8,128)S(1)}, f32[3,8,64,128]{3,2,1,0:T(8,128)}, u32[]{:S(2)}) %copy-start.1) | copy-done | bytes 786456
  4.7 0.0 copy-start.2
  4.7 1.1 %copy-done.2 = f32[3,8,64,128]{3,2,1,0:T(8,128)S(1)} copy-done((f32[3,8,64,128]{3,2,1,0:T(8,128)S(1)}, f32[3,8,64,128]{3,2,1,0:T(8,128)}, u32[]{:S(2)}) %copy-start.2) | copy-done | bytes 786456
  5.8 0.0 copy-start.3
  5.8 1.1 %copy-done.3 = f32[3,8,64,128]{3,2,1,0:T(8,128)S(1)} copy-done((f32[3,8,64,128]{3,2,1,0:T(8,128)S(1)}, f32[3,8,64,128]{3,2,1,0:T(8,128)}, u32[]{:S(2)}) %copy-start.3) | copy-done | bytes 786456
  6.9 0.0 copy-start.4
  6.9 0.9 %copy-done.4 = f32[8,64,128]{2,1,0:T(8,128)S(1)} copy-done((f32[8,64,128]{2,1,0:T(8,128)S(1)}, f32[8,64,128]{2,1,0:T(8,128)}, u32[]{:S(2)}) %copy-start.4) | copy-done | bytes 262168
  7.9 0.0 copy-start.5
  7.9 0.9 %copy-done.5 = f32[2,8,3,8,64]{4,3,2,1,0:T(8,128)S(1)} copy-done((f32[2,8,3,8,64]{4,3,2,1,0:T(8,128)S(1)}, f32[2,8,3,8,64]{4,3,2,1,0:T(8,128)}, u32[]{:S(2)}) %copy-start.5) | copy-done | bytes 98328
  8.8 76.6 %shard_map.129 = (f32[8,64]{1,0:T(8,128)S(1)}, f32[8,128]{1,0:T(8,128)S(1)}, f32[3,8,64,128]{3,2,1,0:T(8,128)S(1)}, f32[3,8,64,128]{3,2,1,0:T(8,128)S(1)}) custom-call(s32[1]{0:T(128)S(6)} %copy.27.floor_ref, s32[1,8]{1,0:T(1,128)S(1)} %copy-done.7, f32[8,4]{1,0:T(8,128)S(1)} %get-tuple-element.13.cos_ref, f32[8,4]{1,0:T(8,128)S(1)} %get-tuple-element.12.sin_ref, ...), custom_call_target="tpu_custom_call" | custom-call | tf_op jit(solution)/shard_map/pallas_call | solution.py:449
  85.4 0.6 slice_reduce_fusion
  86.1 0.6 copy.28
  86.6 0.9 copy.29
  87.5 0.9 copy.30
  (4 shorter events, 0.0 us)
Async XLA Ops:
  0.6 0.7 copy-start.8
  1.7 0.7 copy-start.6
  1.7 0.7 copy-start.7
  2.4 1.1 %copy-start = (f32[3,8,64,128]{3,2,1,0:T(8,128)S(1)}, f32[3,8,64,128]{3,2,1,0:T(8,128)}, u32[]{:S(2)}) copy-start(f32[3,8,64,128]{3,2,1,0:T(8,128)} %e_in.1) | copy-start | bytes 2359300
  3.5 1.1 %copy-start.1 = (f32[3,8,64,128]{3,2,1,0:T(8,128)S(1)}, f32[3,8,64,128]{3,2,1,0:T(8,128)}, u32[]{:S(2)}) copy-start(f32[3,8,64,128]{3,2,1,0:T(8,128)} %h_in.1) | copy-start | bytes 2359300
  4.7 1.1 %copy-start.2 = (f32[3,8,64,128]{3,2,1,0:T(8,128)S(1)}, f32[3,8,64,128]{3,2,1,0:T(8,128)}, u32[]{:S(2)}) copy-start(f32[3,8,64,128]{3,2,1,0:T(8,128)} %ae_in.1) | copy-start | bytes 2359300
  5.8 1.1 %copy-start.3 = (f32[3,8,64,128]{3,2,1,0:T(8,128)S(1)}, f32[3,8,64,128]{3,2,1,0:T(8,128)}, u32[]{:S(2)}) copy-start(f32[3,8,64,128]{3,2,1,0:T(8,128)} %ah_in.1) | copy-start | bytes 2359300
  6.9 0.9 %copy-start.4 = (f32[8,64,128]{2,1,0:T(8,128)S(1)}, f32[8,64,128]{2,1,0:T(8,128)}, u32[]{:S(2)}) copy-start(f32[8,64,128]{2,1,0:T(8,128)} %eps_in.1) | copy-start | bytes 786436
  7.9 0.9 %copy-start.5 = (f32[2,8,3,8,64]{4,3,2,1,0:T(8,128)S(1)}, f32[2,8,3,8,64]{4,3,2,1,0:T(8,128)}, u32[]{:S(2)}) copy-start(f32[2,8,3,8,64]{4,3,2,1,0:T(8,128)} %target_ref.1) | copy-start | bytes 294916

commit v2 on v1

--- a/solution.py
+++ b/solution.py
@@ -30,8 +30,8 @@
     floor_ref, tiles_ref, cos_ref, sin_ref, pair_ref, design_ref, target_ref,
     e_in, h_in, ae_in, ah_in, eps_in,
     grad_ref, weights_ref, e_out, ae_out,
-    es, hs, eps, scale, hx, hy, plane, planes_t, source, sens, mis,
-    fx, fy, part_x, part_y, gbuf,
+    es, hs, eps, scale, hx, hy, plane, planes_t, sens, mis,
+    fx, near_scale, near_source, reply, reply_t, part_x, part_y, gbuf,
     in_sem, out_sem, ssem, rsem, fsend, frecv, psend, precv,
 ):
     gx = lax.axis_index("gx")
@@ -51,11 +51,24 @@
     hx[...] = jnp.zeros_like(hx)
     hy[...] = jnp.zeros_like(hy)
     fx[...] = jnp.zeros_like(fx)
-    fy[...] = jnp.zeros_like(fy)
+    near_scale[...] = jnp.zeros_like(near_scale)
+    near_source[...] = jnp.zeros_like(near_source)
+    reply[...] = jnp.zeros_like(reply)
     for k in range(1, nx):
         pl.semaphore_signal(barrier, inc=1, device_id=(lax.rem(gx + k, nx), gy), device_id_type=MESH)
     for k in range(1, ny):
         pl.semaphore_signal(barrier, inc=1, device_id=(gx, lax.rem(gy + k, ny)), device_id_type=MESH)
+
+    corners = [(dx, dy) for dx in (-1, 1) for dy in (-1, 1)]
+    around = [(-1, 0), (1, 0), (0, -1), (0, 1)] + corners
+
+    def there(dx, dy):
+        return (gx + dx >= 0) & (gx + dx < nx) & (gy + dy >= 0) & (gy + dy < ny)
+
+    for dx, dy in corners:
+        @when(there(dx, dy))
+        def _():
+            pl.semaphore_signal(barrier, inc=1, device_id=(gx + dx, gy + dy), device_id_type=MESH)
 
     row = lax.broadcasted_iota(jnp.int32, (ry, nz), 0)
     lane = lax.broadcasted_iota(jnp.int32, (ry, nz), 1)
@@ -69,10 +82,10 @@
             src, layer, rows, dx, dy = es.at[run, t], 0, pl.ds(0, 8), gx - 1, gy - 1
         else:
             src, layer, rows, dx, dy = hs.at[run, t + 1], rx - 1, pl.ds(ry - 8, 8), gx + 1, gy + 1
-        in_x = pltpu.make_async_remote_copy(
+        in_x = lambda: pltpu.make_async_remote_copy(
             src.at[pl.ds(1, 2), layer], hx.at[slot], ssem.at[slot, 0], rsem.at[slot, 0],
             device_id=(dx, gy), device_id_type=MESH)
-        in_y = [
+        in_y = lambda: [
             pltpu.make_async_remote_copy(
                 src.at[2 * j, :, rows], hy.at[slot, j], ssem.at[slot, 1 + j], rsem.at[slot, 1 + j],
                 device_id=(gx, dy), device_id_type=MESH)
@@ -86,32 +99,32 @@
     def send_x(run, t, kind):
         @when((low, high)[kind][0])
         def _():
-            copies(run, t, kind)[0].start()
+            copies(run, t, kind)[0]().start()
 
     def send_y(run, t, kind):
         @when((low, high)[kind][1])
         def _():
-            for copy in copies(run, t, kind)[1]:
+            for copy in copies(run, t, kind)[1]():
                 copy.start()
 
     def receive(run, t, kind):
         @when((high, low)[kind][0])
         def _():
-            copies(run, t, kind)[0].wait_recv()
+            copies(run, t, kind)[0]().wait_recv()
 
         @when((high, low)[kind][1])
         def _():
-            for copy in copies(run, t, kind)[1]:
+            for copy in copies(run, t, kind)[1]():
                 copy.wait_recv()
 
     def finish(run, t, kind):
         @when((low, high)[kind][0])
         def _():
-            copies(run, t, kind)[0].wait_send()
+            copies(run, t, kind)[0]().wait_send()
 
         @when((low, high)[kind][1])
         def _():
-            for copy in copies(run, t, kind)[1]:
+            for copy in copies(run, t, kind)[1]():
                 copy.wait_send()
 
     def next_y(v, face):
@@ -146,13 +159,13 @@
             h_layer(run, t, i, es[run, t, 1, i + 1], es[run, t, 2, i + 1])
             return carry
 
-        lax.fori_loop(0, rx - 1, inner, 0)
+        lax.fori_loop(0, rx - 1, inner, 0, unroll=True)
         send_y(run, t, 1)
 
     def column(t, c, i):
         return lane == (c * STEPS + t) * rx + i
 
-    def e_layer(run, t, i, hy_last, hz_last, sourced):
+    def e_layer(run, t, i, hy_last, hz_last):
         slot = run * 2 * STEPS + 2 * t + 1
         mx, my, mz = (hs[run, t + 1, c, i] for c in range(3))
         face_x, face_z = hy[slot, 0, i, 7:8, :], hy[slot, 1, i, 7:8, :]
@@ -163,26 +176,20 @@
             es[run, t, 2, i] + s * ((my - hy_last) - (mx - last_y(mx, face_x))),
         ]
         for c in range(3):
-            if sourced:
-                new[c] = new[c] + source_term(t, c, i)
             es[run, t + 1, c, i] = new[c]
 
-    def source_term(t, c, i):
-        value = jnp.sum(jnp.where(column(t, c, i), source[...], 0.0), axis=1, keepdims=True)
-        return jnp.where(at_monitor, value, 0.0)
-
-    def e_step(run, t, sourced, send):
+    def e_step(run, t, send):
         slot = run * 2 * STEPS + 2 * t + 1
         receive(run, t, 1)
-        e_layer(run, t, 0, hx[slot, 0], hx[slot, 1], sourced)
+        e_layer(run, t, 0, hx[slot, 0], hx[slot, 1])
         if send:
             send_x(run, t + 1, 0)
 
         def inner(i, carry):
-            e_layer(run, t, i, hs[run, t + 1, 1, i - 1], hs[run, t + 1, 2, i - 1], sourced)
+            e_layer(run, t, i, hs[run, t + 1, 1, i - 1], hs[run, t + 1, 2, i - 1])
             return carry
 
-        lax.fori_loop(1, rx, inner, 0)
+        lax.fori_loop(1, rx, inner, 0, unroll=True)
         if send:
             send_y(run, t + 1, 0)
 
@@ -195,75 +202,68 @@
             plane[...] = total
             return carry
 
-        lax.fori_loop(0, rx, one, 0)
-
-    def swaps(which):
-        def along(buf, sems, send_to):
-            return [
-                pltpu.make_async_remote_copy(
-                    buf.at[which, 1], buf.at[which, 2 - 2 * j], fsend.at[which, sems, j],
-                    frecv.at[which, sems, j], device_id=send_to[j], device_id_type=MESH)
-                for j in range(2)
-            ]
-
-        return (along(fx, 0, ((gx - 1, gy), (gx + 1, gy))), along(fy, 1, ((gx, gy - 1), (gx, gy + 1))))
-
-    def swap_start(which, a):
-        for j in range(2):
-            @when((low, high)[j][a])
+        lax.fori_loop(0, rx, one, 0, unroll=True)
+
+    def spread_copy(buf, which, n):
+        dx, dy = around[n]
+        return pltpu.make_async_remote_copy(
+            buf.at[1, 1], buf.at[1 - dx, 1 - dy], fsend.at[which, n], frecv.at[which, n],
+            device_id=(gx + dx, gy + dy), device_id_type=MESH)
+
+    def spread(buf, which):
+        for n, (dx, dy) in enumerate(around):
+            @when(there(dx, dy))
             def _():
-                swaps(which)[a][j].start()
-
-    def swap_wait(which, a):
-        for j in range(2):
-            @when((high, low)[j][a])
+                spread_copy(buf, which, n).start()
+
+    def gathered(buf, which):
+        for n, (dx, dy) in enumerate(around):
+            @when(there(-dx, -dy))
             def _():
-                swaps(which)[a][j].wait_recv()
-
-            @when((low, high)[j][a])
+                spread_copy(buf, which, n).wait_recv()
+
+            @when(there(dx, dy))
             def _():
-                swaps(which)[a][j].wait_send()
+                spread_copy(buf, which, n).wait_send()
 
     plane_lane = lax.broadcasted_iota(jnp.int32, (rx, LANES), 1)
 
-    def filter_start(which, value):
-        fx[which, 1] = value
-        swap_start(which, 0)
-
-    def filter_middle(which):
-        swap_wait(which, 0)
-        wide = jnp.concatenate([fx[which, 0], fx[which, 1], fx[which, 2]], 0)
+    def widen(block):
+        rows = []
+        for a in range(3):
+            below = pltpu.roll(block(a, 0), LANES - ry, 1)
+            above = pltpu.roll(block(a, 2), ry, 1)
+            rows.append(jnp.where(plane_lane < ry, block(a, 1),
+                        jnp.where(plane_lane < ry + 4, above,
+                        jnp.where(plane_lane >= LANES - 4, below, 0.0))))
+        return jnp.concatenate(rows, 0)
+
+    def smooth(wide):
         taps = [wide[rx - 2 + d: 2 * rx - 2 + d] for d in range(5)]
-        fy[which, 1] = (taps[0] + 2.0 * taps[1] + 3.0 * taps[2] + 2.0 * taps[3] + taps[4]) / 9.0
-        swap_start(which, 1)
-
-    def filter_end(which):
-        swap_wait(which, 1)
-        below = pltpu.roll(fy[which, 0], LANES - ry, 1)
-        above = pltpu.roll(fy[which, 2], ry, 1)
-        wide = jnp.where(plane_lane < ry, fy[which, 1],
-                         jnp.where(plane_lane < ry + 2, above,
-                                   jnp.where(plane_lane >= LANES - 2, below, 0.0)))
-        taps = [wide if d == 2 else pltpu.roll(wide, (2 - d) % LANES, 1) for d in range(5)]
+        first = (taps[0] + 2.0 * taps[1] + 3.0 * taps[2] + 2.0 * taps[3] + taps[4]) / 9.0
+        taps = [first if d == 2 else pltpu.roll(first, (2 - d) % LANES, 1) for d in range(5)]
         return (taps[0] + 2.0 * taps[1] + 3.0 * taps[2] + 2.0 * taps[3] + taps[4]) / 9.0
 
-    pl.semaphore_wait(barrier, nx - 1 + ny - 1)
+    beside_x = (gx > 0).astype(jnp.int32) + (gx < nx - 1).astype(jnp.int32)
+    beside_y = (gy > 0).astype(jnp.int32) + (gy < ny - 1).astype(jnp.int32)
+    pl.semaphore_wait(barrier, nx - 1 + ny - 1 + beside_x * beside_y)
     gbuf[...] = jnp.zeros_like(gbuf)
     gbuf[0:rx, 0:ry] = design_ref[...]
-    filter_start(0, gbuf[0:rx, :])
+    fx[0, 1, 1] = gbuf[0:rx, :]
+    spread(fx.at[0], 0)
     plane[...] = jnp.zeros_like(plane)
     sens[...] = jnp.zeros_like(sens)
     for run in range(2):
         loads[run].wait()
         send_x(run, 0, 0)
         send_y(run, 0, 0)
-    filter_middle(0)
     loads[2].wait()
     h_step(0, 0)
     loads[3].wait()
     h_step(1, 0)
 
-    filtered = filter_end(0)
+    gathered(fx.at[0], 0)
+    filtered = smooth(widen(lambda a, b: fx[0, a, b]))
     tilted = jnp.tanh(sharpness * (filtered - threshold))
     offset_tanh = jnp.tanh(jnp.full((1, 1), sharpness * threshold, F32))
     projected = (offset_tanh + tilted) / (2.0 * offset_tanh)
@@ -283,19 +283,35 @@
         permittivity = jnp.where(in_slab & (value > 0.0), value, eps[i])
         scale[i] = courant / permittivity
 
-    e_step(0, 0, False, True)
-    e_step(1, 0, False, False)
+    e_step(0, 0, True)
+    e_step(1, 0, True)
     watch(0)
 
-    def forward(t, carry):
+    reach = STEPS - 1
+    spans = 2 * reach + 1
+    z_low = z0 + DZ - reach
+    total = jnp.zeros((ry, nz), F32)
+    for j in range(spans):
+        for i in range(rx):
+            value = jnp.sum(jnp.where(lane == z_low + j, scale[i], 0.0), axis=1, keepdims=True)
+            total = jnp.where(lane == j * rx + i, value, total)
+    planes_t[...] = jnp.transpose(total)
+    for j in range(spans):
+        near_scale[1, 1, j, :, 0:ry] = planes_t[j * rx: (j + 1) * rx, :]
+    spread(near_scale, 2)
+
+    def both(t, carry):
         h_step(0, t)
-        e_step(0, t, False, True)
+        h_step(1, t)
+        e_step(0, t, True)
+        e_step(1, t, True)
         watch(t)
         return carry
 
-    lax.fori_loop(1, STEPS - 1, forward, 0)
+    lax.fori_loop(1, STEPS - 1, both, 0)
     h_step(0, STEPS - 1)
-    e_step(0, STEPS - 1, False, False)
+    h_step(1, STEPS - 1)
+    e_step(0, STEPS - 1, False)
     watch(STEPS - 1)
     stores = [pltpu.make_async_copy(es.at[0, STEPS], e_out, out_sem.at[0]),
               pltpu.make_async_copy(es.at[1, STEPS], ae_out, out_sem.at[1])]
@@ -334,19 +350,25 @@
                 device_id=(other, gy) if axis == 0 else (gx, other), device_id_type=MESH))
         return out
 
-    def gather_sum(buf, axis, value):
-        me, n = (gx, nx) if axis == 0 else (gy, ny)
-        buf[me] = value
+    def gather_start(buf, axis, value):
+        buf[(gx, gy)[axis]] = value
         for copy in gathers(buf, axis):
             copy.start()
+
+    def gather_sum(buf, axis):
         for copy in gathers(buf, axis):
             copy.wait()
         total = buf[0]
-        for k in range(1, n):
+        for k in range(1, (nx, ny)[axis]):
             total = total + buf[k]
         return total
 
-    loss_sums = gather_sum(part_y, 1, gather_sum(part_x, 0, part))
+    gather_start(part_x, 0, part)
+    e_step(1, STEPS - 1, False)
+    gather_start(part_y, 1, gather_sum(part_x, 0))
+    gathered(near_scale, 2)
+    scales = [widen(lambda a, b: near_scale[a, b, j]) for j in range(spans)]
+    loss_sums = gather_sum(part_y, 1)
     losses = loss_sums / float(3 * rx * nx * ry * ny) + 1e-06
     squared = losses * losses
     weights = squared / jnp.sum(squared, axis=0, keepdims=True)
@@ -360,22 +382,84 @@
             im = w * mis[1, k, c]
             for t in range(STEPS):
                 sources[c][t] = sources[c][t] + (cos_ref[k, t] * re - sin_ref[k, t] * im)
-    planes_t[...] = jnp.zeros_like(planes_t)
     for c in range(3):
         for t in range(STEPS):
-            first = (c * STEPS + t) * rx
-            planes_t[first: first + rx, :] = sources[c][t]
-    source[...] = jnp.transpose(planes_t[...])
+            near_source[1, 1, t * 3 + c, :, 0:ry] = sources[c][t]
+    spread(near_source, 3)
     mixed = jnp.sum(weights * pair_ref[...], axis=0, keepdims=True)
 
-    def first_source(i, carry):
+    gathered(near_source, 3)
+    shape = (3 * rx, LANES)
+    wide_row = lax.broadcasted_iota(jnp.int32, shape, 0)
+    wide_lane = lax.broadcasted_iota(jnp.int32, shape, 1)
+    on_grid = ((wide_row >= rx) | (gx > 0)) & ((wide_lane < LANES - 4) | (gy > 0))
+    nothing = jnp.zeros(shape, F32)
+    electric = [[nothing] * (spans + 2) for _ in range(3)]
+    magnetic = [[nothing] * (spans + 2) for _ in range(3)]
+
+    def up_x(v):
+        return pltpu.roll(v, 3 * rx - 1, 0) - v
+
+    def up_y(v):
+        return pltpu.roll(v, LANES - 1, 1) - v
+
+    def down_x(v):
+        return v - pltpu.roll(v, 1, 0)
+
+    def down_y(v):
+        return v - pltpu.roll(v, 1, 1)
+
+    for t in range(STEPS):
+        ex, ey, ez = electric
+        for j in range(reach - t + 1, reach + t + 1):
+            curls = (
+                up_y(ez[j]) - (ey[j + 1] - ey[j]),
+                (ex[j + 1] - ex[j]) - up_x(ez[j]),
+                up_x(ey[j]) - up_y(ex[j]),
+            )
+            for c in range(3):
+                magnetic[c][j] = jnp.where(on_grid, magnetic[c][j] - courant * curls[c], 0.0)
+        mx, my, mz = magnetic
+        for j in range(reach - t + 1, reach + t + 2):
+            if t > 0:
+                s = scales[j - 1]
+                curls = (
+                    down_y(mz[j]) - (my[j] - my[j - 1]),
+                    (mx[j] - mx[j - 1]) - down_x(mz[j]),
+                    down_x(my[j]) - down_y(mx[j]),
+                )
+                for c in range(3):
+                    electric[c][j] = electric[c][j] + s * curls[c]
+            for c in range(3):
+                if j == reach + 1:
+                    electric[c][j] = electric[c][j] + widen(lambda a, b: near_source[a, b, t * 3 + c])
+                first = (j - 1) * rx
+                reply[t * 3 + c, first: first + rx, :] = electric[c][j][rx: 2 * rx, :]
+
+    def turn(n):
+        return jnp.concatenate([reply[n, pl.ds(i, 8, stride=rx), :] for i in range(rx)], 0)
+
+    for n in range(0, 3 * STEPS, 2):
+        pair = jnp.concatenate([turn(n), turn(n + 1)], 0)
+        reply_t[n // 2] = jnp.transpose(pair)[0:ry, :]
+    reached = (lane >= z_low) & (lane < z_low + spans)
+
+    def add_reply(t):
         for c in range(3):
-            es[1, 1, c, i] = es[1, 1, c, i] + source_term(0, c, i)
-        return carry
-
-    lax.fori_loop(0, rx, first_source, 0)
-    send_x(1, 1, 0)
-    send_y(1, 1, 0)
+            n = t * 3 + c
+            for i in range(rx):
+                shift = lax.rem(z_low - ((n % 2) * 8 * rx + 8 * i) + 2 * LANES, LANES)
+                extra = pltpu.roll(reply_t[n // 2], shift, 1)
+                es[1, t + 1, c, i] = es[1, t + 1, c, i] + jnp.where(reached, extra, 0.0)
+
+    for run in range(2):
+        for t in range(STEPS):
+            for kind in range(2):
+                finish(run, t, kind)
+    add_reply(STEPS - 1)
+    stores[1].start()
+    for t in range(STEPS - 1):
+        add_reply(t)
 
     def correlate(s):
         lane_row = lax.broadcasted_iota(jnp.int32, (1, LANES), 1)
@@ -394,21 +478,10 @@
             sens[i] = total
             return carry
 
-        lax.fori_loop(0, rx, one, 0)
-
-    correlate(0)
-
-    def adjoint(t, carry):
-        h_step(1, t)
-        e_step(1, t, True, True)
-        correlate(t)
-        return carry
-
-    lax.fori_loop(1, STEPS - 1, adjoint, 0)
-    h_step(1, STEPS - 1)
-    e_step(1, STEPS - 1, True, False)
-    stores[1].start()
-    correlate(STEPS - 1)
+        lax.fori_loop(0, rx, one, 0, unroll=True)
+
+    for s in range(STEPS):
+        correlate(s)
 
     total = jnp.zeros((ry, nz), F32)
     for i in range(rx):
@@ -417,14 +490,11 @@
     gbuf[...] = jnp.zeros_like(gbuf)
     gbuf[:, 0:ry] = jnp.transpose(total)
     density = gbuf[0:rx, :] / float(3 * DZ)
-    filter_start(1, slope * density)
-    filter_middle(1)
-    grad_ref[...] = filter_end(1)[:, 0:ry]
-
-    for run in range(2):
-        for t in range(STEPS):
-            for kind in range(2):
-                finish(run, t, kind)
+    fx[1, 1, 1] = slope * density
+    spread(fx.at[1], 1)
+    gathered(fx.at[1], 1)
+    grad_ref[...] = smooth(widen(lambda a, b: fx[1, a, b]))[:, 0:ry]
+
     for store in stores:
         store.wait()
 
@@ -443,7 +513,7 @@
     pairs = jnp.pad(pairs.reshape(nf, STEPS * STEPS), ((0, 0), (0, LANES - STEPS * STEPS)))
     smem = pl.BlockSpec(memory_space=pltpu.SMEM)
     vmem = pl.BlockSpec(memory_space=pltpu.VMEM)
-    hbm = pl.BlockSpec(memory_space=pl.ANY)
+    hbm = pl.BlockSpec(memory_space=pltpu.HBM)
     field = jax.ShapeDtypeStruct((3, rx, ry, nz), F32)
     slots = 4 * STEPS
     grad, weights, e_final, adj_e_final = pl.pallas_call(
@@ -465,11 +535,13 @@
             pltpu.VMEM((slots, 2, rx, 8, nz), F32),
             pltpu.VMEM((ry, LANES), F32),
             pltpu.VMEM((LANES, ry), F32),
-            pltpu.VMEM((ry, LANES), F32),
             pltpu.VMEM((rx, ry, nz), F32),
             pltpu.VMEM((2, nf, 3, rx, ry), F32),
-            pltpu.VMEM((2, 3, rx, LANES), F32),
-            pltpu.VMEM((2, 3, rx, LANES), F32),
+            pltpu.VMEM((2, 3, 3, rx, LANES), F32),
+            pltpu.VMEM((3, 3, 2 * STEPS - 1, rx, LANES), F32),
+            pltpu.VMEM((3, 3, 3 * STEPS, rx, LANES), F32),
+            pltpu.VMEM((3 * STEPS, 8 * rx, LANES), F32),
+            pltpu.VMEM((3 * STEPS // 2, ry, LANES), F32),
             pltpu.VMEM((nx, nf, LANES), F32),
             pltpu.VMEM((ny, nf, LANES), F32),
             pltpu.VMEM((LANES, LANES), F32),
@@ -477,13 +549,13 @@
             pltpu.SemaphoreType.DMA((2,)),
             pltpu.SemaphoreType.DMA((slots, 3)),
             pltpu.SemaphoreType.DMA((slots, 3)),
-            pltpu.SemaphoreType.DMA((2, 2, 2)),
-            pltpu.SemaphoreType.DMA((2, 2, 2)),
+            pltpu.SemaphoreType.DMA((4, 8)),
+            pltpu.SemaphoreType.DMA((4, 8)),
             pltpu.SemaphoreType.DMA((2, max(nx, ny))),
             pltpu.SemaphoreType.DMA((2, max(nx, ny))),
         ],
         compiler_params=pltpu.CompilerParams(
-            collective_id=0, has_side_effects=True, vmem_limit_bytes=48 << 20
+            collective_id=0, has_side_effects=True, vmem_limit_bytes=62 << 20
         ),
     )(
         design_floor, design_tiles, cosines, sines, pairs, design, target,

time: 88.8 us -> 75.1 us (0.85)
  Pallas kernels: 76.6 us -> 67.1 us
  local copies, waits for them, and re-layouts: 10.3 us -> 6.27 us
    pallas_call x1, Pallas kernels: 76.6 us -> 67.1 us  [body(): pl.pallas_call(functools.partial(kernel, nx, ny, nf, rx, ry, nz), out_sha...]
    unnamed x21 -> x15, local copies, waits for them, and re-layouts: 9.45 us -> 4.82 us
where the time goes in v2:
time: 75.1 us; the launch traced here: 74.9 us
  Pallas kernels  67.1 us (89%)
  local copies, waits for them, and re-layouts  6.27 us (8%)
  between operations  1.36 us (2%)
    pallas_call x1, Pallas kernels, body(): pl.pallas_call(functools.partial(kernel, nx, ny, nf, rx, ry, nz), out_sha...  67.1 us
    unnamed x15, local copies, waits for them, and re-layouts  4.82 us

profile of v2, /device:TPU:1, one launch (start us, length us, event | category | flops | bytes accessed | tf_op | source)
XLA Modules:
  0.0 74.9 jit_solution(10586974289804281230)
XLA Ops:
  0.6 0.0 copy-start.5
  1.3 0.0 copy-done.5
  1.3 0.1 multiply_sine_fusion
  1.4 0.0 copy-start.1
  1.5 0.0 copy-start.2
  1.5 0.1 copy.21
  1.5 0.5 copy-done.1
  2.0 0.0 copy-done.2
  2.1 0.1 copy.19
  2.1 0.1 copy.23
  2.2 0.6 pad.4.pair_ref
  2.8 67.1 %shard_map.129 = (f32[8,64]{1,0:T(8,128)}, f32[8,128]{1,0:T(8,128)}, f32[3,8,64,128]{3,2,1,0:T(8,128)}, f32[3,8,64,128]{3,2,1,0:T(8,128)}) custom-call(s32[1]{0:T(128)S(6)} %copy.27.floor_ref, s32[1,8]{1,0:T(1,128)} %tiles_ref.1, f32[8,4]{1,0:T(8,128)} %copy-done.2, f32[8,4]{1,0:T(8,128)} %copy-done.1, f32[8,128]{1,0:T(8,128)} %pad.4.pair_ref, ...), custom_call_target="tpu_custom_call" | custom-call | tf_op jit(solution)/shard_map/pallas_call | solution.py:519
  69.9 0.0 copy-start.3
  69.9 0.0 copy-start.4
  69.9 0.7 copy-done.3
  70.6 0.6 slice_reduce_fusion
  71.2 0.0 copy-done.4
  71.2 0.6 copy.28
  71.8 0.0 copy-start
  71.8 2.2 %copy.29 = f32[3,8,64,128]{3,2,1,0:T(8,128)} copy(f32[3,8,64,128]{3,2,1,0:T(8,128)} %get-tuple-element.20) | data formatting | bytes 1572864
  74.0 0.0 copy-done
  74.0 0.9 %copy.30 = f32[3,8,64,128]{3,2,1,0:T(8,128)} copy(f32[3,8,64,128]{3,2,1,0:T(8,128)S(1)} %copy-done) | data formatting | bytes 1572864
  (3 shorter events, 0.0 us)
Async XLA Ops:
  0.6 0.7 copy-start.5
  1.4 0.6 copy-start.1
  1.5 0.6 copy-start.2
  69.9 0.7 copy-start.3
  69.9 1.3 %copy-start.4 = (f32[8,64]{1,0:T(8,128)S(1)}, f32[8,64]{1,0:T(8,128)}, u32[]{:S(2)}) copy-start(f32[8,64]{1,0:T(8,128)} %get-tuple-element.18) | copy-start | bytes 6148
  71.8 2.2 %copy-start = (f32[3,8,64,128]{3,2,1,0:T(8,128)S(1)}, f32[3,8,64,128]{3,2,1,0:T(8,128)}, u32[]{:S(2)}) copy-start(f32[3,8,64,128]{3,2,1,0:T(8,128)} %get-tuple-element.21) | copy-start | bytes 2359300

commit v3 on v2

--- a/solution.py
+++ b/solution.py
@@ -31,7 +31,7 @@
     e_in, h_in, ae_in, ah_in, eps_in,
     grad_ref, weights_ref, e_out, ae_out,
     es, hs, eps, scale, hx, hy, plane, planes_t, sens, mis,
-    fx, near_scale, near_source, reply, reply_t, part_x, part_y, gbuf,
+    fx, near_scale, near_source, last_source, reply, reply_t, part_x, part_y, gbuf,
     in_sem, out_sem, ssem, rsem, fsend, frecv, psend, precv,
 ):
     gx = lax.axis_index("gx")
@@ -53,6 +53,7 @@
     fx[...] = jnp.zeros_like(fx)
     near_scale[...] = jnp.zeros_like(near_scale)
     near_source[...] = jnp.zeros_like(near_source)
+    last_source[...] = jnp.zeros_like(last_source)
     reply[...] = jnp.zeros_like(reply)
     for k in range(1, nx):
         pl.semaphore_signal(barrier, inc=1, device_id=(lax.rem(gx + k, nx), gy), device_id_type=MESH)
@@ -228,15 +229,26 @@
 
     plane_lane = lax.broadcasted_iota(jnp.int32, (rx, LANES), 1)
 
-    def widen(block):
+    def widen(block, half=0):
+        def at(v, moved):
+            return pltpu.roll(v, ry, 1) if moved else v
+
         rows = []
         for a in range(3):
-            below = pltpu.roll(block(a, 0), LANES - ry, 1)
-            above = pltpu.roll(block(a, 2), ry, 1)
-            rows.append(jnp.where(plane_lane < ry, block(a, 1),
+            below = at(block(a, 0), half == 0)
+            above = at(block(a, 2), half == 0)
+            rows.append(jnp.where(plane_lane < ry, at(block(a, 1), half == 1),
                         jnp.where(plane_lane < ry + 4, above,
                         jnp.where(plane_lane >= LANES - 4, below, 0.0))))
         return jnp.concatenate(rows, 0)
+
+    def pack(buf, planes):
+        planes = planes + [jnp.zeros((rx, ry), F32)] * (len(planes) % 2)
+        for n in range(0, len(planes), 2):
+            buf[1, 1, n // 2] = jnp.concatenate([planes[n], planes[n + 1]], 1)
+
+    def unpack(buf, n):
+        return widen(lambda a, b: buf[a, b, n // 2], n % 2)
 
     def smooth(wide):
         taps = [wide[rx - 2 + d: 2 * rx - 2 + d] for d in range(5)]
@@ -296,8 +308,7 @@
             value = jnp.sum(jnp.where(lane == z_low + j, scale[i], 0.0), axis=1, keepdims=True)
             total = jnp.where(lane == j * rx + i, value, total)
     planes_t[...] = jnp.transpose(total)
-    for j in range(spans):
-        near_scale[1, 1, j, :, 0:ry] = planes_t[j * rx: (j + 1) * rx, :]
+    pack(near_scale, [planes_t[j * rx: (j + 1) * rx, :] for j in range(spans)])
     spread(near_scale, 2)
 
     def both(t, carry):
@@ -367,7 +378,7 @@
     e_step(1, STEPS - 1, False)
     gather_start(part_y, 1, gather_sum(part_x, 0))
     gathered(near_scale, 2)
-    scales = [widen(lambda a, b: near_scale[a, b, j]) for j in range(spans)]
+    scales = [unpack(near_scale, j) for j in range(spans)]
     loss_sums = gather_sum(part_y, 1)
     losses = loss_sums / float(3 * rx * nx * ry * ny) + 1e-06
     squared = losses * losses
@@ -382,9 +393,9 @@
             im = w * mis[1, k, c]
             for t in range(STEPS):
                 sources[c][t] = sources[c][t] + (cos_ref[k, t] * re - sin_ref[k, t] * im)
+    pack(near_source, [sources[c][t] for t in range(STEPS - 1) for c in range(3)])
     for c in range(3):
-        for t in range(STEPS):
-            near_source[1, 1, t * 3 + c, :, 0:ry] = sources[c][t]
+        last_source[c, :, 0:ry] = sources[c][STEPS - 1]
     spread(near_source, 3)
     mixed = jnp.sum(weights * pair_ref[...], axis=0, keepdims=True)
 
@@ -432,7 +443,11 @@
                     electric[c][j] = electric[c][j] + s * curls[c]
             for c in range(3):
                 if j == reach + 1:
-                    electric[c][j] = electric[c][j] + widen(lambda a, b: near_source[a, b, t * 3 + c])
+                    if t < STEPS - 1:
+                        added = unpack(near_source, t * 3 + c)
+                    else:
+                        added = jnp.concatenate([nothing[0:rx], last_source[c], nothing[0:rx]], 0)
+                    electric[c][j] = electric[c][j] + added
                 first = (j - 1) * rx
                 reply[t * 3 + c, first: first + rx, :] = electric[c][j][rx: 2 * rx, :]
 
@@ -513,6 +528,7 @@
     pairs = jnp.pad(pairs.reshape(nf, STEPS * STEPS), ((0, 0), (0, LANES - STEPS * STEPS)))
     smem = pl.BlockSpec(memory_space=pltpu.SMEM)
     vmem = pl.BlockSpec(memory_space=pltpu.VMEM)
+    kept = pl.BlockSpec(memory_space=pl.ANY)
     hbm = pl.BlockSpec(memory_space=pltpu.HBM)
     field = jax.ShapeDtypeStruct((3, rx, ry, nz), F32)
     slots = 4 * STEPS
@@ -525,7 +541,7 @@
             field,
         ),
         in_specs=[smem, smem, smem, smem, vmem, vmem, vmem] + [hbm] * 5,
-        out_specs=(vmem, vmem, hbm, hbm),
+        out_specs=(vmem, vmem, kept, kept),
         scratch_shapes=[
             pltpu.VMEM((2, STEPS + 1, 3, rx, ry, nz), F32),
             pltpu.VMEM((2, STEPS + 1, 3, rx, ry, nz), F32),
@@ -538,8 +554,9 @@
             pltpu.VMEM((rx, ry, nz), F32),
             pltpu.VMEM((2, nf, 3, rx, ry), F32),
             pltpu.VMEM((2, 3, 3, rx, LANES), F32),
-            pltpu.VMEM((3, 3, 2 * STEPS - 1, rx, LANES), F32),
-            pltpu.VMEM((3, 3, 3 * STEPS, rx, LANES), F32),
+            pltpu.VMEM((3, 3, STEPS, rx, LANES), F32),
+            pltpu.VMEM((3, 3, (3 * STEPS - 2) // 2, rx, LANES), F32),
+            pltpu.VMEM((3, rx, LANES), F32),
             pltpu.VMEM((3 * STEPS, 8 * rx, LANES), F32),
             pltpu.VMEM((3 * STEPS // 2, ry, LANES), F32),
             pltpu.VMEM((nx, nf, LANES), F32),

time: 75.1 us -> 69.3 us (0.923)
  Pallas kernels: 67.1 us -> 61.4 us
    pallas_call x1, Pallas kernels: 67.1 us -> 61.4 us  [body(): pl.pallas_call(functools.partial(kernel, nx, ny, nf, rx, ry, nz), out_sha...]
where the time goes in v3:
time: 69.3 us; the launch traced here: 69.1 us
  Pallas kernels  61.4 us (89%)
  local copies, waits for them, and re-layouts  6.27 us (9%)
  between operations  1.36 us (2%)
    pallas_call x1, Pallas kernels, body(): pl.pallas_call(functools.partial(kernel, nx, ny, nf, rx, ry, nz), out_sha...  61.4 us
    unnamed x15, local copies, waits for them, and re-layouts  4.82 us

profile of v3, /device:TPU:1, one launch (start us, length us, event | category | flops | bytes accessed | tf_op | source)
XLA Modules:
  0.0 69.1 jit_solution(18282559173113148741)
XLA Ops:
  0.6 0.0 copy-start.5
  1.3 0.0 copy-done.5
  1.3 0.1 multiply_sine_fusion
  1.4 0.0 copy-start.1
  1.5 0.0 copy-start.2
  1.5 0.1 copy.21
  1.5 0.5 copy-done.1
  2.0 0.0 copy-done.2
  2.1 0.1 copy.19
  2.1 0.1 copy.23
  2.2 0.6 pad.4.pair_ref
  2.8 61.4 %shard_map.129 = (f32[8,64]{1,0:T(8,128)}, f32[8,128]{1,0:T(8,128)}, f32[3,8,64,128]{3,2,1,0:T(8,128)}, f32[3,8,64,128]{3,2,1,0:T(8,128)}) custom-call(s32[1]{0:T(128)S(6)} %copy.27.floor_ref, s32[1,8]{1,0:T(1,128)} %tiles_ref.1, f32[8,4]{1,0:T(8,128)} %copy-done.2, f32[8,4]{1,0:T(8,128)} %copy-done.1, f32[8,128]{1,0:T(8,128)} %pad.4.pair_ref, ...), custom_call_target="tpu_custom_call" | custom-call | tf_op jit(solution)/shard_map/pallas_call | solution.py:535
  64.2 0.0 copy-start.3
  64.2 0.0 copy-start.4
  64.2 0.7 copy-done.3
  64.9 0.6 slice_reduce_fusion
  65.5 0.0 copy-done.4
  65.5 0.6 copy.28
  66.1 0.0 copy-start
  66.1 2.2 %copy.29 = f32[3,8,64,128]{3,2,1,0:T(8,128)} copy(f32[3,8,64,128]{3,2,1,0:T(8,128)} %get-tuple-element.20) | data formatting | bytes 1572864
  68.2 0.0 copy-done
  68.2 0.9 %copy.30 = f32[3,8,64,128]{3,2,1,0:T(8,128)} copy(f32[3,8,64,128]{3,2,1,0:T(8,128)S(1)} %copy-done) | data formatting | bytes 1572864
  (3 shorter events, 0.0 us)
Async XLA Ops:
  0.6 0.7 copy-start.5
  1.4 0.6 copy-start.1
  1.5 0.6 copy-start.2
  64.2 0.7 copy-start.3
  64.2 1.3 %copy-start.4 = (f32[8,64]{1,0:T(8,128)S(1)}, f32[8,64]{1,0:T(8,128)}, u32[]{:S(2)}) copy-start(f32[8,64]{1,0:T(8,128)} %get-tuple-element.18) | copy-start | bytes 6148
  66.1 2.2 %copy-start = (f32[3,8,64,128]{3,2,1,0:T(8,128)S(1)}, f32[3,8,64,128]{3,2,1,0:T(8,128)}, u32[]{:S(2)}) copy-start(f32[3,8,64,128]{3,2,1,0:T(8,128)} %get-tuple-element.21) | copy-start | bytes 2359300
